TPU v7x, 32 devices: a whole 2x2x4 slice. The times are simulated.
32 devices in a mesh: lat: 4 (over z), lon: 8 (over y, x, core).
Axes of the slice: x: 2, y: 2, z: 4, core: 2. Of those that a mesh axis runs over, the one named last changes fastest.
Arguments:
- ensemble: float32 [128, 128, 8, 256], P('lat', 'lon'), may hold values from -6 to 6
- obs_values: float32 [3, 256], replicated, may hold values from -8 to 8
- obs_noise: float32 [3, 256, 256], replicated, may hold values from -6 to 6
- obs_var: float32 [3, 256], replicated, may hold values from 0.1 to 1
- obs_cells: int32 [3, 256], replicated, may hold values from 0 to 4095, as said below
- owner_tiles: int32 [3, 2], replicated, may hold values from 0 to 7, as said below
- radius: int32 [3], replicated, may hold values from 64 to 128, as said below
- courant_lat: float32 [128, 128, 8], P('lat', 'lon'), may hold values from -0.35 to 0.35
- courant_lon: float32 [128, 128, 8], P('lat', 'lon'), may hold values from -0.35 to 0.35
- diffusivity: float32 [128, 128, 8], P('lat', 'lon'), may hold values from 0.02 to 0.07
Outputs:
- forecast: float32 [128, 128, 8, 256], P('lat', 'lon')
Inputs may be any that keep to these rules, and one draw needn't show every extreme that they name: `obs_cells`: each row holds 256 distinct local cells, the last cell of the tile among them; cell (i, j, k) of a tile has index (i * 16 + j) * 8 + k. `owner_tiles`: row b names a latitude tile below 4 and a longitude tile below 8; consecutive batches' tiles differ by at most one in each (longitude wraps). `radius`: every draw holds both ends.
All inputs are finite; a program needn't handle non-finite values.
Results may differ from a plain program's by a relative error of at most 0.0003.
Values sent between devices are 32-bit elements; how exact they have to be, the bound alone decides.
No kernel may reach another device: no remote copies, remote signals or barrier semaphores. Data moves between devices by JAX's collectives and lax.ppermute only.
A program may use at most 64 MiB of HBM per device.

v0:
```python
import jax
import jax.numpy as jnp
from jax import lax
from jax.sharding import PartitionSpec as P

LEV = 8
NBATCH = 3
CLAT = 32
CLON = 16


def extended(x, sides, width, wrap):
    for axis, dim in sides:
        size, length = (lax.axis_size(axis), x.shape[dim])
        up = [(i, (i + 1) % size) for i in range(size if wrap else size - 1)]
        down = [(j, i) for i, j in up]
        last = lax.slice_in_dim(x, length - width, length, axis=dim)
        first = lax.slice_in_dim(x, 0, width, axis=dim)
        before = lax.ppermute(last, axis, up)
        after = lax.ppermute(first, axis, down)
        x = jnp.concatenate([before, x, after], axis=dim)
    return x


def taper_weight(dist_sq, radius_cells):
    ratio = 1.0 - dist_sq / (radius_cells * radius_cells)
    return jnp.square(jnp.maximum(ratio, 0.0))


def analysis(observed_rows, values, noise, variance):
    members = observed_rows.shape[1]
    spread = observed_rows - jnp.mean(observed_rows, axis=1, keepdims=True)
    covariance = jnp.dot(spread, spread.T, precision=lax.Precision.HIGHEST) / (
        members - 1
    ) + jnp.diag(variance)
    innovation = values[:, None] + jnp.sqrt(variance)[:, None] * noise - observed_rows
    factor = jnp.linalg.cholesky(covariance)
    inner = jax.scipy.linalg.solve_triangular(factor, innovation, lower=True)
    weights = jax.scipy.linalg.solve_triangular(factor, inner, lower=True, trans=1)
    return (spread, weights)


def locality(lat_cells, lon_cells, cells, owner_lat, owner_lon, radius_cells, total_lon):
    position = cells // LEV
    obs_lat = owner_lat * CLAT + position // CLON
    obs_lon = owner_lon * CLON + position % CLON
    lat_gap = (lat_cells[:, None] - obs_lat[None, :]).astype(jnp.float32)
    lon_gap = jnp.abs(lon_cells[:, None] - obs_lon[None, :])
    lon_gap = jnp.minimum(lon_gap, total_lon - lon_gap).astype(jnp.float32)
    dist_sq = jnp.square(lat_gap) + jnp.square(lon_gap)
    return taper_weight(dist_sq, radius_cells.astype(jnp.float32))


def regress(flat_state, spread, weights, weight_map):
    members = flat_state.shape[1]
    places = weight_map.shape[0]
    levels = flat_state.shape[0] // places
    anomaly = flat_state - jnp.mean(flat_state, axis=1, keepdims=True)
    covar = jnp.dot(anomaly, spread.T, precision=lax.Precision.HIGHEST) / (members - 1)
    covar = (covar.reshape(places, levels, -1) * weight_map[:, None, :]).reshape(covar.shape)
    return flat_state + jnp.dot(covar, weights, precision=lax.Precision.HIGHEST)


def advance(padded, lat_speed, lon_speed, spread_rate):
    centre = padded[1:-1, 1:-1]
    below_row = padded[:-2, 1:-1]
    above_row = padded[2:, 1:-1]
    west_col = padded[1:-1, :-2]
    east_col = padded[1:-1, 2:]
    lat_part = lat_speed[..., None]
    lon_part = lon_speed[..., None]
    rate_part = spread_rate[..., None]
    transport = (
        jnp.maximum(lat_part, 0.0) * (centre - below_row)
        + jnp.minimum(lat_part, 0.0) * (above_row - centre)
        + jnp.maximum(lon_part, 0.0) * (centre - west_col)
        + jnp.minimum(lon_part, 0.0) * (east_col - centre)
    )
    return (
        centre
        - transport
        + rate_part * (below_row + above_row + west_col + east_col - 4.0 * centre)
    )


def shards(
    ensemble,
    obs_values,
    obs_noise,
    obs_var,
    obs_cells,
    owner_tiles,
    radius,
    courant_lat,
    courant_lon,
    diffusivity,
):
    lat_index = lax.axis_index("lat")
    lon_index = lax.axis_index("lon")
    lon_count = lax.axis_size("lon")
    total_lon = CLON * lon_count
    members = ensemble.shape[3]
    lat_cells = jnp.broadcast_to(
        (lat_index * CLAT + jnp.arange(CLAT, dtype=jnp.int32))[:, None], (CLAT, CLON)
    ).reshape(-1)
    lon_cells = jnp.broadcast_to(
        (lon_index * CLON + jnp.arange(CLON, dtype=jnp.int32))[None, :], (CLAT, CLON)
    ).reshape(-1)
    flat_state = ensemble.reshape(-1, members)
    for which_batch in range(NBATCH):
        owner_lat = owner_tiles[which_batch, 0]
        owner_lon = owner_tiles[which_batch, 1]
        picked = flat_state[obs_cells[which_batch]]
        is_owner = jnp.logical_and(lat_index == owner_lat, lon_index == owner_lon)
        observed_rows = lax.psum(jnp.where(is_owner, picked, 0.0), ("lat", "lon"))
        spread, weights = analysis(
            observed_rows, obs_values[which_batch], obs_noise[which_batch], obs_var[which_batch]
        )
        weight_map = locality(
            lat_cells,
            lon_cells,
            obs_cells[which_batch],
            owner_lat,
            owner_lon,
            radius[which_batch],
            total_lon,
        )
        flat_state = regress(flat_state, spread, weights, weight_map)
    state = flat_state.reshape(ensemble.shape)
    widened = extended(state, (("lat", 0),), 2, False)
    widened = extended(widened, (("lon", 1),), 2, True)
    stacked = jnp.stack([courant_lat, courant_lon, diffusivity])
    stacked = extended(stacked, (("lat", 1),), 1, False)
    stacked = extended(stacked, (("lon", 2),), 1, True)
    middle = advance(widened, stacked[0], stacked[1], stacked[2])
    state = advance(middle, courant_lat, courant_lon, diffusivity)
    return state


def solution(mesh):
    in_specs = (
        P("lat", "lon", None, None),
        P(),
        P(),
        P(),
        P(),
        P(),
        P(),
        P("lat", "lon", None),
        P("lat", "lon", None),
        P("lat", "lon", None),
    )
    out_specs = P("lat", "lon", None, None)
    return jax.shard_map(shards, mesh=mesh, in_specs=in_specs, out_specs=out_specs, check_vma=False)
```

profile of v0, /device:TPU:0, one launch (start us, length us, event | category | flops | bytes accessed | tf_op | source)
XLA Modules:
  0.0 689.5 jit_solution(12196111616715013765)
XLA Ops:
  8.9 3.2 gather_fusion
  32.7 111.0 %all-reduce.5.cloned.1.call-done = f32[256,256]{0,1:T(8,128)} async-done(((f32[256,256]{0,1:T(8,128)}), f32[256,256]{0,1:T(8,128)}) %all-reduce.5.cloned.1.call-update) | async-done | bytes 262160 | tf_op jit(solution)/shard_map/psum | solution.py:115
  147.9 11.7 %cholesky.172 = f32[128,128]{1,0:T(8,128)S(1)} custom-call(f32[128,128]{1,0:T(8,128)S(1)} %cholesky.270), custom_call_target="Cholesky" | custom-call | tf_op jit(solution)/shard_map/jit(cholesky)/cholesky | solution.py:37
  159.6 9.8 %custom-call.20 = f32[1,128,128]{1,2,0:T(8,128)S(1)} custom-call(f32[1,128,128]{2,1,0:T(8,128)S(1)} %get-tuple-element.127), custom_call_target="InvertDiagBlocksLowerTriangular" | custom-call | tf_op jit(solution)/shard_map/jit(cholesky)/cholesky | solution.py:37
  171.6 11.9 %cholesky.189 = f32[128,128]{1,0:T(8,128)S(1)} custom-call(f32[128,128]{1,0:T(8,128)S(1)} %convolution_subtract_fusion.8), custom_call_target="Cholesky" | custom-call | tf_op jit(solution)/shard_map/jit(cholesky)/cholesky | solution.py:37
  186.3 4.0 while.12
  190.9 19.7 %custom-call.22 = f32[2,128,128]{1,2,0:T(8,128)S(1)} custom-call(f32[2,128,128]{2,1,0:T(8,128)S(1)} %get-tuple-element.49), custom_call_target="InvertDiagBlocksLowerTriangular" | custom-call | tf_op jit(solution)/shard_map/jit(_solve_triangular)/triangular_solve | solution.py:39
  212.5 5.7 fusion.2
  218.2 5.1 fusion.112
  223.3 3.3 gather_fusion.1
  227.9 125.3 %all-reduce.7.cloned.1.call-done = f32[256,256]{0,1:T(8,128)} async-done(((f32[256,256]{0,1:T(8,128)}), f32[256,256]{0,1:T(8,128)}) %all-reduce.7.cloned.1.call-update) | async-done | bytes 262160 | tf_op jit(solution)/shard_map/psum | solution.py:115
  356.2 11.7 %cholesky.206 = f32[128,128]{1,0:T(8,128)S(1)} custom-call(f32[128,128]{1,0:T(8,128)S(1)} %cholesky.273), custom_call_target="Cholesky" | custom-call | tf_op jit(solution)/shard_map/jit(cholesky)/cholesky | solution.py:37
  368.0 9.8 %custom-call.23 = f32[1,128,128]{1,2,0:T(8,128)S(1)} custom-call(f32[1,128,128]{2,1,0:T(8,128)S(1)} %get-tuple-element.123), custom_call_target="InvertDiagBlocksLowerTriangular" | custom-call | tf_op jit(solution)/shard_map/jit(cholesky)/cholesky | solution.py:37
  378.3 11.7 %cholesky.223 = f32[128,128]{1,0:T(8,128)S(1)} custom-call(f32[128,128]{1,0:T(8,128)S(1)} %convolution_subtract_fusion.7), custom_call_target="Cholesky" | custom-call | tf_op jit(solution)/shard_map/jit(cholesky)/cholesky | solution.py:37
  392.7 4.2 while.13
  396.9 19.7 %custom-call.25 = f32[2,128,128]{1,2,0:T(8,128)S(1)} custom-call(f32[2,128,128]{2,1,0:T(8,128)S(1)} %get-tuple-element.51), custom_call_target="InvertDiagBlocksLowerTriangular" | custom-call | tf_op jit(solution)/shard_map/jit(_solve_triangular)/triangular_solve | solution.py:39
  418.5 5.8 fusion.1
  424.3 5.3 fusion.113
  429.6 3.3 gather_fusion.2
  433.8 125.8 %all-reduce.9.cloned.1.call-done = f32[256,256]{0,1:T(8,128)} async-done(((f32[256,256]{0,1:T(8,128)}), f32[256,256]{0,1:T(8,128)}) %all-reduce.9.cloned.1.call-update) | async-done | bytes 262160 | tf_op jit(solution)/shard_map/psum | solution.py:115
  562.5 11.7 %cholesky.240 = f32[128,128]{1,0:T(8,128)S(1)} custom-call(f32[128,128]{1,0:T(8,128)S(1)} %cholesky.276), custom_call_target="Cholesky" | custom-call | tf_op jit(solution)/shard_map/jit(cholesky)/cholesky | solution.py:37
  574.3 9.8 %custom-call.26 = f32[1,128,128]{1,2,0:T(8,128)S(1)} custom-call(f32[1,128,128]{2,1,0:T(8,128)S(1)} %get-tuple-element.119), custom_call_target="InvertDiagBlocksLowerTriangular" | custom-call | tf_op jit(solution)/shard_map/jit(cholesky)/cholesky | solution.py:37
  584.6 11.7 %cholesky.257 = f32[128,128]{1,0:T(8,128)S(1)} custom-call(f32[128,128]{1,0:T(8,128)S(1)} %convolution_subtract_fusion.6), custom_call_target="Cholesky" | custom-call | tf_op jit(solution)/shard_map/jit(cholesky)/cholesky | solution.py:37
  599.2 4.3 while.14
  603.5 19.9 %custom-call.28 = f32[2,128,128]{1,2,0:T(8,128)S(1)} custom-call(f32[2,128,128]{2,1,0:T(8,128)S(1)} %get-tuple-element.53), custom_call_target="InvertDiagBlocksLowerTriangular" | custom-call | tf_op jit(solution)/shard_map/jit(_solve_triangular)/triangular_solve | solution.py:39
  625.3 5.6 fusion
  630.9 3.4 convolution_add_fusion
  634.4 3.4 collective-permute-start
  639.2 4.6 collective-permute-start.4
  658.4 6.3 collective-permute-done.6
  670.6 6.4 multiply_add_fusion
  677.1 5.4 multiply_add_fusion.1
  (225 shorter events, 73.4 us)
Async XLA Ops:
  6.5 9.9 %copy-start.18 = (f32[3,256,256]{2,1,0:T(8,128)S(1)}, f32[3,256,256]{2,1,0:T(8,128)}, u32[]{:S(2)}) copy-start(f32[3,256,256]{2,1,0:T(8,128)} %param.17) | copy-start | bytes 2359300
  6.5 10.0 %copy-start.31 = (f32[3,256]{1,0:T(4,128)S(1)}, f32[3,256]{1,0:T(4,128)}, u32[]{:S(2)}) copy-start(f32[3,256]{1,0:T(4,128)} %param.16) | copy-start | bytes 9220
  6.5 13.2 %copy-start.26 = (s32[3]{0:T(128)S(1)}, s32[3]{0:T(128)}, u32[]{:S(2)}) copy-start(s32[3]{0:T(128)} %param.21) | copy-start | bytes 40
  6.5 137.1 %all-reduce.5.cloned.1.call-start = ((), (), s32[]{:S(2)}) async-start(), calls=%async_computation | async-start | bytes 524288 | tf_op jit(solution)/shard_map/psum | solution.py:115
  12.0 14.4 %copy-start.25 = (s32[3,256]{1,0:T(4,128)S(1)}, s32[3,256]{1,0:T(4,128)}, u32[]{:S(2)}) copy-start(s32[3,256]{1,0:T(4,128)} %param.19) | copy-start | bytes 9220
  14.3 339.0 %all-reduce.7.cloned.1.call-start = ((), (), s32[]{:S(2)}) async-start(), calls=%async_computation.1 | async-start | bytes 524288 | tf_op jit(solution)/shard_map/psum | solution.py:115
  16.4 14.6 %copy-start.24 = (f32[1,256]{1,0:T(1,128)}, f32[1,256]{1,0:T(1,128)S(1)}, u32[]{:S(2)}) copy-start(f32[1,256]{1,0:T(1,128)S(1)} %get-tuple-element.132) | copy-start | bytes 3076
  16.5 14.8 %copy-start.22 = (f32[1,256]{1,0:T(1,128)}, f32[1,256]{1,0:T(1,128)S(1)}, u32[]{:S(2)}) copy-start(f32[1,256]{1,0:T(1,128)S(1)} %get-tuple-element.133) | copy-start | bytes 3076
  16.5 15.5 %copy-start.20 = (f32[1,256]{1,0:T(1,128)}, f32[1,256]{1,0:T(1,128)S(1)}, u32[]{:S(2)}) copy-start(f32[1,256]{1,0:T(1,128)S(1)} %get-tuple-element.131) | copy-start | bytes 3076
  22.3 10.4 %copy-start.14 = (f32[32,16,8]{0,2,1:T(8,128)S(1)}, f32[32,16,8]{0,2,1:T(8,128)}, u32[]{:S(2)}) copy-start(f32[32,16,8]{0,2,1:T(8,128)} %param.24) | copy-start | bytes 49156
  22.3 10.4 %copy-start.15 = (f32[32,16,8]{0,2,1:T(8,128)S(1)}, f32[32,16,8]{0,2,1:T(8,128)}, u32[]{:S(2)}) copy-start(f32[32,16,8]{0,2,1:T(8,128)} %param.23) | copy-start | bytes 49156
  22.3 10.4 %copy-start.16 = (f32[32,16,8]{0,2,1:T(8,128)S(1)}, f32[32,16,8]{0,2,1:T(8,128)}, u32[]{:S(2)}) copy-start(f32[32,16,8]{0,2,1:T(8,128)} %param.22) | copy-start | bytes 49156
  143.7 68.8 %copy-start.5 = (f32[256,256]{0,1:T(8,128)S(1)}, f32[256,256]{0,1:T(8,128)}, u32[]{:S(2)}) copy-start(f32[256,256]{0,1:T(8,128)} %all-reduce.5.cloned.1.call-done) | copy-start | bytes 786436
  218.1 135.1 %copy-start.28 = (f32[256]{0:T(256)S(1)}, f32[256]{0:T(256)}, u32[]{:S(2)}) copy-start(f32[256]{0:T(256)} %sqrt.22) | copy-start | bytes 3076
  218.1 135.1 %copy-start.30 = (f32[1,256]{1,0:T(1,128)S(1)}, f32[1,256]{1,0:T(1,128)}, u32[]{:S(2)}) copy-start(f32[1,256]{1,0:T(1,128)} %get-tuple-element.130) | copy-start | bytes 3076
  223.3 131.1 %copy-start.23 = (f32[1,256]{1,0:T(1,128)S(1)}, f32[1,256]{1,0:T(1,128)}, u32[]{:S(2)}) copy-start(f32[1,256]{1,0:T(1,128)} %copy-done.22) | copy-start | bytes 3076
  223.3 169.4 %copy-start.33 = (s32[2,2]{1,0:T(2,128)S(1)}, s32[2,2]{1,0:T(2,128)}, u32[]{:S(2)}) copy-start(s32[2,2]{1,0:T(2,128)} %copy-done.32) | copy-start | bytes 52
  227.5 332.1 %all-reduce.9.cloned.1.call-start = ((), (), s32[]{:S(2)}) async-start(), calls=%async_computation.2 | async-start | bytes 524288 | tf_op jit(solution)/shard_map/psum | solution.py:115
  353.3 65.2 %copy-start.7 = (f32[256,256]{0,1:T(8,128)S(1)}, f32[256,256]{0,1:T(8,128)}, u32[]{:S(2)}) copy-start(f32[256,256]{0,1:T(8,128)} %all-reduce.7.cloned.1.call-done) | copy-start | bytes 786436
  424.2 135.3 %copy-start.27 = (f32[256]{0:T(256)S(1)}, f32[256]{0:T(256)}, u32[]{:S(2)}) copy-start(f32[256]{0:T(256)} %sqrt.23) | copy-start | bytes 3076
  424.2 135.3 %copy-start.29 = (f32[1,256]{1,0:T(1,128)S(1)}, f32[1,256]{1,0:T(1,128)}, u32[]{:S(2)}) copy-start(f32[1,256]{1,0:T(1,128)} %get-tuple-element.128) | copy-start | bytes 3076
  429.6 131.1 %copy-start.21 = (f32[1,256]{1,0:T(1,128)S(1)}, f32[1,256]{1,0:T(1,128)}, u32[]{:S(2)}) copy-start(f32[1,256]{1,0:T(1,128)} %copy-done.20) | copy-start | bytes 3076
  559.6 65.7 %copy-start.6 = (f32[256,256]{0,1:T(8,128)S(1)}, f32[256,256]{0,1:T(8,128)}, u32[]{:S(2)}) copy-start(f32[256,256]{0,1:T(8,128)} %all-reduce.9.cloned.1.call-done) | copy-start | bytes 786436
  634.3 17.1 %copy-start = (f32[4096,256]{1,0:T(8,128)}, f32[4096,256]{1,0:T(8,128)S(1)}, u32[]{:S(2)}) copy-start(f32[4096,256]{1,0:T(8,128)S(1)} %convolution_add_fusion) | copy-start | bytes 12582916
  634.4 10.7 %collective-permute-start = (f32[2,16,8,256]{3,2,1,0:T(8,128)S(1)}, f32[2,16,8,256]{3,2,1,0:T(8,128)S(1)}, u32[]{:S(2)}, u32[]{:S(2)}) collective-permute-start(f32[2,16,8,256]{3,2,1,0:T(8,128)S(1)} %bitcast.213), channel_id=1, source_target_pairs={{0,8},{8,16},{16,24},{1,9},{9,17},{17,25},{2,10},{10,18},{18,26},{... | collective-permute-start | bytes 786440 | tf_op jit(solution)/shard_map/ppermute | solution.py:19
  637.8 9.1 %collective-permute-start.1 = (f32[2,16,8,256]{3,2,1,0:T(8,128)S(1)}, f32[2,16,8,256]{3,2,1,0:T(8,128)S(1)}, u32[]{:S(2)}, u32[]{:S(2)}) collective-permute-start(f32[2,16,8,256]{3,2,1,0:T(8,128)S(1)} %bitcast.212), channel_id=1, source_target_pairs={{8,0},{16,8},{24,16},{9,1},{17,9},{25,17},{10,2},{18,10},{26,18},{... | collective-permute-start | bytes 786440 | tf_op jit(solution)/shard_map/ppermute | solution.py:20
  639.2 11.4 %collective-permute-start.4 = (f32[3,1,16,8]{1,3,2,0:T(8,128)S(1)}, f32[3,1,16,8]{1,3,2,0:T(8,128)S(1)}, u32[]{:S(2)}, u32[]{:S(2)}) collective-permute-start(f32[3,1,16,8]{1,3,2,0:T(8,128)S(1)} %get-tuple-element.110), channel_id=1, source_target_pairs={{0,8},{8,16},{16,24},{1,9},{9,17},{17,25},{2,10},{10,18},{18,26},{... | collective-permute-start | bytes 4616 | tf_op jit(solution)/shard_map/ppermute | solution.py:19
  643.8 7.6 %collective-permute-start.5 = (f32[3,1,16,8]{1,3,2,0:T(8,128)S(1)}, f32[3,1,16,8]{1,3,2,0:T(8,128)S(1)}, u32[]{:S(2)}, u32[]{:S(2)}) collective-permute-start(f32[3,1,16,8]{1,3,2,0:T(8,128)S(1)} %get-tuple-element.111), channel_id=1, source_target_pairs={{8,0},{16,8},{24,16},{9,1},{17,9},{25,17},{10,2},{18,10},{26,18},{... | collective-permute-start | bytes 4616 | tf_op jit(solution)/shard_map/ppermute | solution.py:20
  648.0 19.0 %collective-permute-start.2 = (f32[36,2,8,256]{3,2,1,0:T(8,128)}, f32[36,2,8,256]{3,2,1,0:T(8,128)S(1)}, u32[]{:S(2)}, u32[]{:S(2)}) collective-permute-start(f32[36,2,8,256]{3,2,1,0:T(8,128)} %get-tuple-element.90), channel_id=1, source_target_pairs={{0,1},{1,2},{2,3},{3,4},{4,5},{5,6},{6,7},{7,0},{8,9},{9,10},{10,1... | collective-permute-start | bytes 1769480 | tf_op jit(solution)/shard_map/ppermute | solution.py:19
  648.0 19.0 %collective-permute-start.3 = (f32[36,2,8,256]{3,2,1,0:T(8,128)}, f32[36,2,8,256]{3,2,1,0:T(8,128)S(1)}, u32[]{:S(2)}, u32[]{:S(2)}) collective-permute-start(f32[36,2,8,256]{3,2,1,0:T(8,128)} %get-tuple-element.91), channel_id=1, source_target_pairs={{1,0},{2,1},{3,2},{4,3},{5,4},{6,5},{7,6},{0,7},{9,8},{10,9},{11,1... | collective-permute-start | bytes 1769480 | tf_op jit(solution)/shard_map/ppermute | solution.py:20
  651.4 13.3 %collective-permute-start.6 = (f32[3,34,1,8]{1,3,2,0:T(8,128)S(1)}, f32[3,34,1,8]{1,3,2,0:T(8,128)S(1)}, u32[]{:S(2)}, u32[]{:S(2)}) collective-permute-start(f32[3,34,1,8]{1,3,2,0:T(8,128)S(1)} %get-tuple-element.97), channel_id=1, source_target_pairs={{0,1},{1,2},{2,3},{3,4},{4,5},{5,6},{6,7},{7,0},{8,9},{9,10},{10,1... | collective-permute-start | bytes 9800 | tf_op jit(solution)/shard_map/ppermute | solution.py:19
  651.5 13.2 %collective-permute-start.7 = (f32[3,34,1,8]{1,3,2,0:T(8,128)S(1)}, f32[3,34,1,8]{1,3,2,0:T(8,128)S(1)}, u32[]{:S(2)}, u32[]{:S(2)}) collective-permute-start(f32[3,34,1,8]{1,3,2,0:T(8,128)S(1)} %get-tuple-element.98), channel_id=1, source_target_pairs={{1,0},{2,1},{3,2},{4,3},{5,4},{6,5},{7,6},{0,7},{9,8},{10,9},{11,1... | collective-permute-start | bytes 9800 | tf_op jit(solution)/shard_map/ppermute | solution.py:20
  (13 other events, 58.2 us)
Sparse Core Ops, SparseCore 0:
  14.4 129.2 all-reduce.4
  227.6 125.6 all-reduce.6
  433.9 125.6 all-reduce.8
where the time goes:
time: 699 us; the launch traced here: 689 us
  waiting for transfers between devices  371 us (53%)
  other arithmetic  191 us (27%)
  matrix products  44.4 us (6%)
  local copies, waits for them, and re-layouts  38.6 us (6%)
  between operations  27.8 us (4%)
  starting transfers between devices  16.4 us (2%)
    psum x3, waiting for transfers between devices, shards(): observed_rows = lax.psum(jnp.where(is_owner, picked, 0.0), ('lat', 'lon'))  362 us
    another operation x20, other arithmetic, analysis(): factor = jnp.linalg.cholesky(covariance)  104 us
    another operation x7, other arithmetic, analysis(): jax.scipy.linalg.solve_triangular(factor, inner, lower=True, trans=1)  59.9 us
    dot_general x3, matrix products, regress(): jnp.dot(anomaly, spread.T, precision=lax.Precision.HIGHEST) / (members - 1)  17 us
  transfers between devices with their start and end apart: 11, of which 6 were waited for; matrix products, arithmetic and copies ran while one was open for 3% of the time, Pallas kernels for 0%

commit v1 on v0

v1 whole, which is shorter than its diff:
```python
import functools

import jax
import jax.numpy as jnp
from jax import lax
from jax.experimental import pallas as pl
from jax.experimental.pallas import tpu as pltpu
from jax.sharding import PartitionSpec as P

NBATCH = 3
CLAT = 32
CLON = 16
HALO = 2
F32 = jnp.float32
BF16 = jnp.bfloat16
VMEM = pl.BlockSpec(memory_space=pltpu.VMEM)


def shifted(x, axis, flip):
    size = lax.axis_size(axis)
    return lax.ppermute(x, axis, [(i, i ^ flip) for i in range(size)])


def stages(axis, first):
    size, out = lax.axis_size(axis), []
    while first < size:
        out.append((axis, first))
        first *= 2
    return out


def everywhere(x):
    sizes = (lax.axis_size("lat"), lax.axis_size("lon"))
    if any(n & (n - 1) for n in sizes) or sizes[1] < 2:
        return lax.psum(x, ("lat", "lon"))
    x = x + shifted(x, "lon", 1)
    core = lax.axis_index("lon") % 2
    half = x.shape[0] // 2
    mine = lax.dynamic_slice_in_dim(x, core * half, half, 0)
    a, b = mine[: half // 2], mine[half // 2 :]
    lon, lat = stages("lon", 2), stages("lat", 1)
    for (a_axis, a_flip), (b_axis, b_flip) in zip(lon + lat, lat + lon):
        a, b = a + shifted(a, a_axis, a_flip), b + shifted(b, b_axis, b_flip)
    mine = jnp.concatenate([a, b])
    other = shifted(mine, "lon", 1)
    return jnp.where(
        core == 0, jnp.concatenate([mine, other]), jnp.concatenate([other, mine])
    )


def taper(lat_a, lon_a, lat_b, lon_b, radius, total_lon):
    lat_gap = (lat_a[:, None] - lat_b[None, :]).astype(F32)
    lon_gap = jnp.abs(lon_a[:, None] - lon_b[None, :])
    lon_gap = jnp.minimum(lon_gap, total_lon - lon_gap).astype(F32)
    radius = radius.astype(F32)
    ratio = 1.0 - (jnp.square(lat_gap) + jnp.square(lon_gap)) / (radius * radius)
    return jnp.square(jnp.maximum(ratio, 0.0))


def split(x):
    high = x.astype(BF16)
    return high, (x - high.astype(F32)).astype(BF16)


def exact_dot(a, b):
    return jnp.dot(a, b, precision=lax.Precision.HIGHEST, preferred_element_type=F32)


def split_dot(a, b_high, *b_rest):
    high, low = split(a)
    dot = functools.partial(jnp.dot, preferred_element_type=F32)
    total = dot(high, b_high) + dot(low, b_high)
    for b in b_rest:
        total = total + dot(high, b)
    return total


def eliminate(strips):
    shape = strips[0].shape
    lane = lax.broadcasted_iota(jnp.int32, shape, 1)
    row = lax.broadcasted_iota(jnp.int32, shape, 0)
    block = lane < 8
    first = strips[0]
    diag = [jnp.broadcast_to(first[:, c : c + 1], shape) for c in range(8)]
    scaled = jnp.where(block, jnp.where(lane == row, 1.0, 0.0), first)
    for k in range(8):
        pivot = 1.0 / jnp.broadcast_to(diag[k][k : k + 1], shape)
        here = row == k
        for c in range(k + 1, 8):
            top = jnp.broadcast_to(diag[c][k : k + 1], shape) * pivot
            diag[c] = jnp.where(here, top, diag[c] - diag[k] * top)
        top = jnp.broadcast_to(scaled[k : k + 1], shape) * pivot
        scaled = jnp.where(here, top, scaled - diag[k] * top)
    rows = [jnp.broadcast_to(scaled[c : c + 1], shape) for c in range(8)]
    out = []
    for strip in strips[1:]:
        terms = [jnp.broadcast_to(strip[:, c : c + 1], shape) * rows[c] for c in range(8)]
        while len(terms) > 1:
            terms = [terms[j] + terms[j + 1] for j in range(0, len(terms), 2)]
        out.append(jnp.where(block, 0.0, strip) - terms[0])
    out.append(scaled)
    return tuple(pltpu.roll(strip, shape[1] - 8, 1) for strip in out)


def inverse(a):
    size = a.shape[0]
    strips = tuple(a[8 * i : 8 * i + 8] for i in range(size // 8))
    strips = lax.fori_loop(0, size // 8, lambda _, s: eliminate(s), strips)
    return jnp.concatenate(strips, axis=0)


def solve_kernel(
    rows_ref, target_ref, var_ref, mutual_ref, st_high, st_low, w_high, w_mid, w_low, y_ref
):
    count, nobs, members = rows_ref.shape
    half = nobs // 2
    y_ref[...] = rows_ref[...]
    diagonal = lax.broadcasted_iota(jnp.int32, (nobs, nobs), 0) == lax.broadcasted_iota(
        jnp.int32, (nobs, nobs), 1
    )

    @pl.loop(0, count)
    def _(b):
        y = y_ref[b]
        spread = y - jnp.sum(y, axis=1, keepdims=True) / members
        spread_t = spread.T
        high, low = split(spread_t)
        st_high[b] = high
        st_low[b] = low
        cov = exact_dot(spread, spread_t) / (members - 1)
        cov = cov + jnp.where(diagonal, jnp.broadcast_to(var_ref[b], (nobs, nobs)), 0.0)
        right = target_ref[b] - y
        lower = cov[half:, :half]
        upper = jnp.concatenate([cov[:half, half:], right[:half]], axis=1)
        upper = exact_dot(inverse(cov[:half, :half]), upper)
        rest = exact_dot(lower, upper)
        schur = inverse(cov[half:, half:] - rest[:, :half])
        w_second = exact_dot(schur, right[half:] - rest[:, half:])
        w_first = upper[:, half:] - exact_dot(upper[:, :half], w_second)
        w = jnp.concatenate([w_first, w_second], axis=0)
        high, mid = split(w)
        w_high[b] = high
        w_mid[b] = mid
        w_low[b] = (w - high.astype(F32) - mid.astype(F32)).astype(BF16)

        @pl.loop(b + 1, count)
        def _(later):
            y_later = y_ref[later]
            gain = exact_dot(y_later, spread_t) * mutual_ref[b + later - 1]
            y_ref[later] = y_later + exact_dot(gain, w)


def solve(rows, target, variance, mutual):
    count, nobs, members = rows.shape
    out = [jax.ShapeDtypeStruct((count, members, nobs), BF16)] * 2
    out += [jax.ShapeDtypeStruct((count, nobs, members), BF16)] * 3
    return pl.pallas_call(
        solve_kernel,
        out_shape=out,
        in_specs=[VMEM] * 4,
        out_specs=[VMEM] * 5,
        scratch_shapes=[pltpu.VMEM((count, nobs, members), F32)],
        compiler_params=pltpu.CompilerParams(vmem_limit_bytes=60 << 20),
    )(rows, target, variance[:, None, :], mutual)


def sweep(source, coef_ref, i, width, coef_row, coef_col, store):
    rows = [[source[i + d, j] for j in range(width + 2)] if d == 1 else None for d in range(3)]
    for j in range(width):
        near = (rows[1][j + 1], source[i, j + 1], source[i + 2, j + 1], rows[1][j], rows[1][j + 2])
        total = None
        for n, part in enumerate(near):
            coef = coef_ref[n, coef_row, coef_col + j]
            coef = jnp.concatenate([coef] * (part.shape[-1] // coef.shape[-1]), axis=-1)
            total = part * coef if total is None else total + part * coef
        store(j, total)


def move_kernel(chunk, *refs):
    pieces, refs = refs[:5], refs[5:]
    taper_hbm, coef_hbm, st_high, st_low, w_high, w_mid, w_low = refs[:7]
    out_hbm, x_ref, taper_ref, coef_ref, z_ref, out_ref, sems, out_sem = refs[7:]
    count = st_high.shape[0]
    tall, wide, levels, members = x_ref.shape
    inner = (pl.ds(HALO, tall - 2 * HALO), pl.ds(HALO, wide - 2 * HALO))
    places = (
        inner,
        (pl.ds(0, HALO), inner[1]),
        (pl.ds(tall - HALO, HALO), inner[1]),
        (slice(None), pl.ds(0, HALO)),
        (slice(None), pl.ds(wide - HALO, HALO)),
    )
    copies = [
        pltpu.make_async_copy(piece, x_ref.at[place], sems.at[n])
        for n, (piece, place) in enumerate(zip(pieces, places))
    ]
    copies.append(pltpu.make_async_copy(taper_hbm, taper_ref, sems.at[5]))
    coef_copy = pltpu.make_async_copy(coef_hbm, coef_ref, sems.at[6])
    for copy in copies:
        copy.start()
    coef_copy.start()
    for copy in copies:
        copy.wait()

    @pl.loop(0, tall // chunk)
    def _(i):
        at = pl.ds(i * chunk, chunk)
        x = x_ref[at].reshape(chunk * wide * levels, members)
        for b in range(count):
            gain = split_dot(x, st_high[b], st_low[b]).reshape(chunk * wide, levels, -1)
            gain = gain * taper_ref[b, at].reshape(chunk * wide, -1)[:, None, :]
            gain = gain.reshape(chunk * wide * levels, -1)
            x = x + split_dot(gain, w_high[b], w_mid[b], w_low[b])
        x_ref[at] = x.reshape(chunk, wide, levels, members)

    coef_copy.wait()

    @pl.loop(0, tall - 2)
    def _(i):
        def store(j, value):
            z_ref[i, j] = value

        sweep(x_ref, coef_ref, i, wide - 2, i + 1, 1, store)

    @pl.loop(0, tall - 4)
    def _(i):
        def store(j, value):
            out_ref[i, j] = value

        sweep(z_ref, coef_ref, i, wide - 4, i + 2, 2, store)
        pltpu.make_async_copy(out_ref.at[i], out_hbm.at[i], out_sem).start()

    pltpu.make_async_copy(out_ref, out_hbm, out_sem).wait()


def move(pieces, tapers, coefs, spread_t, weights):
    wide, (tall, _, levels, members) = pieces[0].shape[1] + 2 * HALO, pieces[3].shape
    hbm = pl.BlockSpec(memory_space=pl.ANY)
    return pl.pallas_call(
        functools.partial(move_kernel, 4 if tall % 4 == 0 else 1),
        out_shape=jax.ShapeDtypeStruct(pieces[0].shape, F32),
        in_specs=[hbm] * 7 + [VMEM] * 5,
        out_specs=hbm,
        scratch_shapes=[
            pltpu.VMEM((tall, wide, levels, members), F32),
            pltpu.VMEM(tapers.shape, F32),
            pltpu.VMEM(coefs.shape, F32),
            pltpu.VMEM((tall - 2, wide - 2, levels, members), F32),
            pltpu.VMEM(pieces[0].shape, F32),
            pltpu.SemaphoreType.DMA((7,)),
            pltpu.SemaphoreType.DMA,
        ],
        compiler_params=pltpu.CompilerParams(vmem_limit_bytes=60 << 20),
    )(*pieces, tapers, coefs, *spread_t, *weights)


def packed(x, extra):
    width = x.shape[-1]
    extra = extra.reshape(-1)
    tail = -(-extra.shape[0] // (8 * width)) * 8
    extra = jnp.pad(extra, (0, tail * width - extra.shape[0])).reshape(tail, width)
    return jnp.concatenate([x.reshape(-1, width), extra])


def unpacked(rows, shape, extra_shape):
    count = 1
    for n in shape[:-1]:
        count *= n
    size = 1
    for n in extra_shape:
        size *= n
    return rows[:count].reshape(shape), rows[count:].reshape(-1)[:size].reshape(extra_shape)


def edges(x, extra, axis, dim, wrap):
    size, length = lax.axis_size(axis), x.shape[dim]
    up = [(i, (i + 1) % size) for i in range(size if wrap else size - 1)]
    down = [(j, i) for i, j in up]
    found = []
    for pairs, at in ((up, length - HALO), (down, 0)):
        edge = lax.slice_in_dim(x, at, at + HALO, axis=dim)
        last = extra.shape[dim + 1] - 1 if at else 0
        thin = lax.slice_in_dim(extra, last, last + 1, axis=dim + 1)
        got = lax.ppermute(packed(edge, thin), axis, pairs)
        found.append(unpacked(got, edge.shape, thin.shape))
    return found


def shards(
    ensemble,
    obs_values,
    obs_noise,
    obs_var,
    obs_cells,
    owner_tiles,
    radius,
    courant_lat,
    courant_lon,
    diffusivity,
):
    lat_index = lax.axis_index("lat")
    lon_index = lax.axis_index("lon")
    total_lon = CLON * lax.axis_size("lon")
    levels, members = ensemble.shape[2:]
    nobs = obs_cells.shape[1]

    mine = jnp.logical_and(owner_tiles[:, 0] == lat_index, owner_tiles[:, 1] == lon_index)
    rows = ensemble.reshape(-1, members)[obs_cells.reshape(-1)]
    rows = jnp.where(jnp.repeat(mine, nobs)[:, None], rows, 0.0)
    rows = everywhere(rows).reshape(NBATCH, nobs, members)

    stacked = jnp.stack([courant_lat, courant_lon, diffusivity])
    (south, south_thin), (north, north_thin) = edges(ensemble, stacked, "lat", 0, False)
    rows, south, north = lax.optimization_barrier((rows, south, north))
    stacked = jnp.concatenate([south_thin, stacked, north_thin], axis=1)
    columns = jnp.concatenate(
        [
            jnp.concatenate([part[:, :HALO], part[:, -HALO:]], axis=1)
            for part in (south, ensemble, north)
        ]
    )
    (west, west_thin), (east, east_thin) = edges(columns, stacked, "lon", 1, True)
    stacked = jnp.concatenate([west_thin, stacked, east_thin], axis=2)
    tall, wide = west.shape[0], ensemble.shape[1] + 2 * HALO
    stacked = jnp.pad(stacked, ((0, 0), (1, 1), (1, 1), (0, 0)))
    lat_speed, lon_speed, rate = stacked
    coefs = jnp.stack(
        [
            1.0 - jnp.abs(lat_speed) - jnp.abs(lon_speed) - 4.0 * rate,
            jnp.maximum(lat_speed, 0.0) + rate,
            rate - jnp.minimum(lat_speed, 0.0),
            jnp.maximum(lon_speed, 0.0) + rate,
            rate - jnp.minimum(lon_speed, 0.0),
        ]
    )
    coefs = jnp.broadcast_to(coefs[..., None], coefs.shape + (128,))

    place = obs_cells // levels
    obs_lat = owner_tiles[:, :1] * CLAT + place // CLON
    obs_lon = owner_tiles[:, 1:] * CLON + place % CLON
    lat_cells = lat_index * CLAT - HALO + jnp.arange(tall, dtype=jnp.int32)
    lon_cells = lon_index * CLON - HALO + jnp.arange(wide, dtype=jnp.int32)
    lon_cells = (lon_cells + total_lon) % total_lon
    lat_cells = jnp.broadcast_to(lat_cells[:, None], (tall, wide)).reshape(-1)
    lon_cells = jnp.broadcast_to(lon_cells[None, :], (tall, wide)).reshape(-1)
    tapers = jnp.stack(
        [
            taper(lat_cells, lon_cells, obs_lat[b], obs_lon[b], radius[b], total_lon)
            for b in range(NBATCH)
        ]
    ).reshape(NBATCH, tall, wide, nobs) / (members - 1)
    mutual = jnp.stack(
        [
            taper(obs_lat[c], obs_lon[c], obs_lat[b], obs_lon[b], radius[b], total_lon)
            for b, c in ((0, 1), (0, 2), (1, 2))
        ]
    ) / (members - 1)
    target = obs_values[:, :, None] + jnp.sqrt(obs_var)[:, :, None] * obs_noise

    factors = solve(rows, target, obs_var, mutual)
    pieces = (ensemble, south, north, west, east)
    return move(pieces, tapers, coefs, factors[:2], factors[2:])


def solution(mesh):
    cells = P("lat", "lon", None)
    in_specs = (P("lat", "lon", None, None),) + (P(),) * 6 + (cells,) * 3
    out_specs = P("lat", "lon", None, None)
    return jax.shard_map(
        shards, mesh=mesh, in_specs=in_specs, out_specs=out_specs, check_vma=False
    )
```

time: 699 us -> 181 us (0.26); the launches traced: 689 us -> 180 us
  waiting for transfers between devices: 371 us -> 26.7 us
  other arithmetic: 191 us -> 15.3 us
  Pallas kernels: 0 us -> 87.8 us
  matrix products: 44.4 us -> 0 us
  between operations: 27.8 us -> 2.59 us
  local copies, waits for them, and re-layouts: 38.6 us -> 28.1 us
    psum x3 -> x0, waiting for transfers between devices: 362 us -> none  [shards(): observed_rows = lax.psum(jnp.where(is_owner, picked, 0.0), ('lat', 'lon'))]
    another operation x27 -> x1, other arithmetic: 164 us -> 0.01 us  [shards(): jnp.stack([1.0 - jnp.abs(lat_speed) - jnp.abs(lon_speed) - 4.0 * rate, jn...]
    pallas_call x0 -> x2, Pallas kernels: none -> 87.8 us  [the longest x1 48.9 us: solve(): pl.pallas_call(solve_kernel, out_shape=out, in_specs=[VMEM] * 4, out_spec...]
    dot_general x9 -> x0, matrix products: 35.8 us -> none  [the longest x3 17 us: regress(): jnp.dot(anomaly, spread.T, precision=lax.Precision.HIGHEST) / (members - 1)]
    ppermute x8 -> x14, waiting for transfers between devices: 8.81 us -> 26.7 us  [the longest x10 26.7 us: shifted(): return lax.ppermute(x, axis, [(i, i ^ flip) for i in range(size)])]
    another operation x28 -> x1, local copies, waits for them, and re-layouts: 12.9 us -> 0.95 us  [shards(): jnp.stack([1.0 - jnp.abs(lat_speed) - jnp.abs(lon_speed) - 4.0 * rate, jn...]
    add x7 -> x12, other arithmetic: 11.9 us -> 1.53 us  [the longest x1 1.18 us: shards(): target = obs_values[:, :, None] + jnp.sqrt(obs_var)[:, :, None] * obs_noise]
    slice x7 -> x24, local copies, waits for them, and re-layouts: 3.73 us -> 13.7 us  [the longest x4 4.93 us: unpacked(): rows[:count].reshape(shape)]
  transfers between devices with their start and end apart: 11 -> 14, of which waited for: 6 -> 7; matrix products, arithmetic and copies ran while one was open for 3% -> 13% of each run, Pallas kernels for 0% -> 27%
where the time goes in v1:
time: 181 us; the launch traced here: 180 us
  Pallas kernels  87.8 us (49%)
  local copies, waits for them, and re-layouts  28.1 us (16%)
  waiting for transfers between devices  26.7 us (15%)
  starting transfers between devices  19.9 us (11%)
  other arithmetic  15.3 us (8%)
  between operations  2.59 us (1%)
    pallas_call x1, Pallas kernels, solve(): pl.pallas_call(solve_kernel, out_shape=out, in_specs=[VMEM] * 4, out_spec...  48.9 us
    pallas_call x1, Pallas kernels, move(): pl.pallas_call(functools.partial(move_kernel, 4 if tall % 4 == 0 else 1),...  38.9 us
    ppermute x10, waiting for transfers between devices, shifted(): return lax.ppermute(x, axis, [(i, i ^ flip) for i in range(size)])  26.7 us
    ppermute x10, starting transfers between devices, shifted(): return lax.ppermute(x, axis, [(i, i ^ flip) for i in range(size)])  10.5 us
    ppermute x4, starting transfers between devices, edges(): got = lax.ppermute(packed(edge, thin), axis, pairs)  9.37 us
    broadcast_in_dim x1, local copies, waits for them, and re-layouts, shards(): coefs = jnp.broadcast_to(coefs[..., None], coefs.shape + (128,))  5.64 us
    slice x4, local copies, waits for them, and re-layouts, unpacked(): rows[:count].reshape(shape)  4.93 us
    slice x10, local copies, waits for them, and re-layouts, unpacked(): rows[count:].reshape(-1)[:size].reshape(extra_shape)  4.37 us
  transfers between devices with their start and end apart: 14, of which 7 were waited for; matrix products, arithmetic and copies ran while one was open for 13% of the time, Pallas kernels for 27%

profile of v1, /device:TPU:0, one launch (start us, length us, event | category | flops | bytes accessed | tf_op | source)
XLA Modules:
  0.0 180.4 jit_solution(6811922919073337513)
XLA Ops:
  1.6 4.3 %gather_fusion = f32[768,256]{1,0:T(8,128)S(1)} fusion(f32[4096,256]{1,0:T(8,128)} %bitcast.42, s32[1024]{0:T(1024)S(1)} %pad_clamp_fusion), kind=kCustom, calls=%fused_computation | custom fusion | bytes 1575936 | tf_op jit(solution)/shard_map/gather | solution.py:308
  7.1 1.1 fusion.53
  9.0 5.2 %collective-permute-start.10 = (f32[264,256]{1,0:T(8,128)}, f32[264,256]{1,0:T(8,128)}, u32[]{:S(2)}, u32[]{:S(2)}) collective-permute-start(f32[264,256]{1,0:T(8,128)} %pad_maximum_fusion.3), channel_id=1, source_target_pairs={{0,8},{8,16},{16,24},{1,9},{9,17},{17,25},{2,10},{10,18},{18,26},{... | collective-permute-start | bytes 811016 | tf_op jit(solution)/shard_map/ppermute | solution.py:284
  15.0 1.3 collective-permute-start.11
  19.0 1.6 collective-permute-start.1
  20.6 2.6 %collective-permute-start.5 = (f32[192,256]{1,0:T(8,128)S(1)}, f32[192,256]{1,0:T(8,128)S(1)}, u32[]{:S(2)}, u32[]{:S(2)}) collective-permute-start(f32[192,256]{1,0:T(8,128)S(1)} %get-tuple-element.34), channel_id=1, source_target_pairs={{0,8},{8,0},{16,24},{24,16},{1,9},{9,1},{17,25},{25,17},{2,10},{10... | collective-permute-start | bytes 589832 | tf_op jit(solution)/shard_map/ppermute | solution.py:21
  23.3 2.9 %collective-permute-done.1 = f32[192,256]{1,0:T(8,128)S(1)} collective-permute-done((f32[192,256]{1,0:T(8,128)S(1)}, f32[192,256]{1,0:T(8,128)S(1)}, u32[]{:S(2)}, u32[]{:S(2)}) %collective-permute-start.1) | collective-permute-done | bytes 196640 | tf_op jit(solution)/shard_map/ppermute | solution.py:21
  26.1 3.8 %collective-permute-done.5 = f32[192,256]{1,0:T(8,128)S(1)} collective-permute-done((f32[192,256]{1,0:T(8,128)S(1)}, f32[192,256]{1,0:T(8,128)S(1)}, u32[]{:S(2)}, u32[]{:S(2)}) %collective-permute-start.5) | collective-permute-done | bytes 196640 | tf_op jit(solution)/shard_map/ppermute | solution.py:21
  30.0 1.6 collective-permute-start.2
  31.5 1.9 %collective-permute-start.6 = (f32[192,256]{1,0:T(8,128)S(1)}, f32[192,256]{1,0:T(8,128)S(1)}, u32[]{:S(2)}, u32[]{:S(2)}) collective-permute-start(f32[192,256]{1,0:T(8,128)S(1)} %get-tuple-element.32), channel_id=1, source_target_pairs={{0,16},{8,24},{16,0},{24,8},{1,17},{9,25},{17,1},{25,9},{2,18},{10... | collective-permute-start | bytes 589832 | tf_op jit(solution)/shard_map/ppermute | solution.py:21
  33.5 2.7 %collective-permute-done.2 = f32[192,256]{1,0:T(8,128)S(1)} collective-permute-done((f32[192,256]{1,0:T(8,128)S(1)}, f32[192,256]{1,0:T(8,128)S(1)}, u32[]{:S(2)}, u32[]{:S(2)}) %collective-permute-start.2) | collective-permute-done | bytes 196640 | tf_op jit(solution)/shard_map/ppermute | solution.py:21
  36.3 5.3 %collective-permute-done.6 = f32[192,256]{1,0:T(8,128)S(1)} collective-permute-done((f32[192,256]{1,0:T(8,128)S(1)}, f32[192,256]{1,0:T(8,128)S(1)}, u32[]{:S(2)}, u32[]{:S(2)}) %collective-permute-start.6) | collective-permute-done | bytes 196640 | tf_op jit(solution)/shard_map/ppermute | solution.py:21
  41.6 1.6 collective-permute-start.7
  43.2 2.5 %collective-permute-done.3 = f32[192,256]{1,0:T(8,128)S(1)} collective-permute-done((f32[192,256]{1,0:T(8,128)S(1)}, f32[192,256]{1,0:T(8,128)S(1)}, u32[]{:S(2)}, u32[]{:S(2)}) %collective-permute-start.3) | collective-permute-done | bytes 196640 | tf_op jit(solution)/shard_map/ppermute | solution.py:21
  45.8 2.7 %collective-permute-done.7 = f32[192,256]{1,0:T(8,128)S(1)} collective-permute-done((f32[192,256]{1,0:T(8,128)S(1)}, f32[192,256]{1,0:T(8,128)S(1)}, u32[]{:S(2)}, u32[]{:S(2)}) %collective-permute-start.7) | collective-permute-done | bytes 196640 | tf_op jit(solution)/shard_map/ppermute | solution.py:21
  49.7 6.9 %collective-permute-done.4 = f32[192,256]{1,0:T(8,128)S(1)} collective-permute-done((f32[192,256]{1,0:T(8,128)S(1)}, f32[192,256]{1,0:T(8,128)S(1)}, u32[]{:S(2)}, u32[]{:S(2)}) %collective-permute-start.4) | collective-permute-done | bytes 196640 | tf_op jit(solution)/shard_map/ppermute | solution.py:21
  58.1 1.4 fusion.27
  59.5 2.1 %fusion.52 = (f32[32,2,8,256]{3,2,1,0:T(8,128)S(1)}, f32[32,2,8,256]{3,2,1,0:T(8,128)}) fusion(f32[32,16,8,256]{3,2,1,0:T(8,128)} %refs_0_.1), kind=kLoop, calls=%fused_computation.119 | loop fusion | bytes 2097152 | tf_op jit(solution)/shard_map/slice | solution.py:318
  65.0 1.0 copy.13
  67.1 1.0 slice.204
  68.1 1.1 slice.206
  69.2 2.4 %maximum_select_fusion = f32[768,256]{1,0:T(8,128)} fusion(f32[384,256]{1,0:T(8,128)} %collective-permute-done.9, f32[192,256]{1,0:T(8,128)} %copy-done.3, f32[192,256]{1,0:T(8,128)} %copy-done.2, pred[]{:T(512)S(6)} %eq.23), kind=kLoop, calls=%fused_computation.27 | loop fusion | flops 983040 | bytes 1572865 | tf_op jit(solution)/shard_map/jit(_where)/select_n | solution.py:46
  71.8 0.9 pad_maximum_fusion
  73.2 1.8 maximum_multiply_fusion.refs_5_
  75.9 2.4 %collective-permute-start.13 = (f32[584,256]{1,0:T(8,128)S(1)}, f32[584,256]{1,0:T(8,128)S(1)}, u32[]{:S(2)}, u32[]{:S(2)}) collective-permute-start(f32[584,256]{1,0:T(8,128)S(1)} %pad_maximum_fusion.1), channel_id=1, source_target_pairs={{1,0},{2,1},{3,2},{4,3},{5,4},{6,5},{7,6},{0,7},{9,8},{10,9},{11,1... | collective-permute-start | bytes 1794056 | tf_op jit(solution)/shard_map/ppermute | solution.py:284
  78.2 2.1 %maximum_multiply_fusion.1.mutual_ref = f32[3,256,256]{2,1,0:T(8,128)} fusion(f32[1,256,256]{2,1,0:T(8,128)} %get-tuple-element.48, f32[1,256,256]{2,1,0:T(8,128)} %get-tuple-element.49, f32[1,256,256]{2,1,0:T(8,128)} %get-tuple-element.47), kind=kLoop, calls=%fused_computation.28 | loop fusion | flops 589824 | bytes 1572864 | tf_op jit(solution)/shard_map/div | solution.py:352
  80.4 1.2 multiply_add_fusion.target_ref
  81.5 48.9 %shard_map.100 = (bf16[3,256,256]{2,1,0:T(8,128)(2,1)}, bf16[3,256,256]{2,1,0:T(8,128)(2,1)}, bf16[3,256,256]{2,1,0:T(8,128)(2,1)}, bf16[3,256,256]{2,1,0:T(8,128)(2,1)}, bf16[3,256,256]{2,1,0:T(8,128)(2,1)}) custom-call(f32[3,256,256]{2,1,0:T(8,128)} %bitcast.43, f32[3,256,256]{2,1,0:T(8,128)} %multiply_add_fusion.target_ref, ...), custom_call_target="tpu_custom_call" | custom-call | tf_op jit(solution)/shard_map/pallas_call | solution.py:157
  131.9 1.0 copy.18
  132.9 2.0 %slice.212 = f32[576,256]{1,0:T(8,128)} slice(f32[584,256]{1,0:T(8,128)} %collective-permute-done.12), slice={[0:576], [0:256]} | slice | bytes 1179648 | tf_op jit(solution)/shard_map/slice | solution.py:272
  135.7 5.6 %broadcast_in_dim.24.refs_6_ = f32[5,36,20,8,128]{4,3,2,1,0:T(8,128)} broadcast(f32[5,36,20,8]{3,2,1,0:T(8,128)S(1)} %copy.18), dimensions={0,1,2,3} | broadcast | bytes 14860800 | tf_op jit(solution)/shard_map/broadcast_in_dim | solution.py:336
  141.4 38.9 %shard_map.101 = f32[32,16,8,256]{3,2,1,0:T(8,128)} custom-call(f32[32,16,8,256]{3,2,1,0:T(8,128)} %refs_0_.1, f32[2,16,8,256]{3,2,1,0:T(8,128)} %bitcast.49, f32[2,16,8,256]{3,2,1,0:T(8,128)} %bitcast.51, f32[36,2,8,256]{3,2,1,0:T(8,128)} %bitcast.46, f32[36,2,8,256]{3,2,1,0:T(8,128)} %bitcast.47, f32[3,36,20,256]{3,2,1,0:T(8,128)} %maximum_multiply_fusion.refs_5_, ...), custom_call_target="tpu_custom_call" | custom-call | tf_op jit(solution)/shard_map/pallas_call | solution.py:239
  (120 shorter events, 16.3 us)
Async XLA Ops:
  1.6 5.1 %copy-start.7 = (f32[32,16,8]{0,2,1:T(8,128)S(1)}, f32[32,16,8]{0,2,1:T(8,128)}, u32[]{:S(2)}) copy-start(f32[32,16,8]{0,2,1:T(8,128)} %param.19) | copy-start | bytes 49156
  1.6 5.1 %copy-start.8 = (f32[32,16,8]{0,2,1:T(8,128)S(1)}, f32[32,16,8]{0,2,1:T(8,128)}, u32[]{:S(2)}) copy-start(f32[32,16,8]{0,2,1:T(8,128)} %param.18) | copy-start | bytes 49156
  1.6 5.1 %copy-start.10 = (f32[32,16,8]{0,2,1:T(8,128)S(1)}, f32[32,16,8]{0,2,1:T(8,128)}, u32[]{:S(2)}) copy-start(f32[32,16,8]{0,2,1:T(8,128)} %param.17) | copy-start | bytes 49156
  6.0 10.4 %copy-start.14 = (s32[3]{0:T(128)S(1)}, s32[3]{0:T(128)}, u32[]{:S(2)}) copy-start(s32[3]{0:T(128)} %param.16) | copy-start | bytes 40
  6.2 17.1 %copy-start.16 = (s32[3,2]{0,1:T(2,128)S(1)}, s32[3,2]{0,1:T(2,128)}, u32[]{:S(2)}) copy-start(s32[3,2]{0,1:T(2,128)} %param.15) | copy-start | bytes 76
  6.2 12.8 %collective-permute-start = (f32[768,256]{1,0:T(8,128)S(1)}, f32[768,256]{1,0:T(8,128)S(1)}, u32[]{:S(2)}, u32[]{:S(2)}) collective-permute-start(f32[768,256]{1,0:T(8,128)S(1)} %broadcast_select_fusion), channel_id=1, source_target_pairs={{0,1},{1,0},{2,3},{3,2},{4,5},{5,4},{6,7},{7,6},{8,9},{9,8},{10,11... | collective-permute-start | bytes 2359304 | tf_op jit(solution)/shard_map/ppermute | solution.py:21
  7.1 26.3 %copy-start.12 = (s32[3,256]{1,0:T(4,128)S(1)}, s32[3,256]{1,0:T(4,128)}, u32[]{:S(2)}) copy-start(s32[3,256]{1,0:T(4,128)} %param.14) | copy-start | bytes 9220
  9.0 52.6 %collective-permute-start.10 = (f32[264,256]{1,0:T(8,128)}, f32[264,256]{1,0:T(8,128)}, u32[]{:S(2)}, u32[]{:S(2)}) collective-permute-start(f32[264,256]{1,0:T(8,128)} %pad_maximum_fusion.3), channel_id=1, source_target_pairs={{0,8},{8,16},{16,24},{1,9},{9,17},{17,25},{2,10},{10,18},{18,26},{... | collective-permute-start | bytes 811016 | tf_op jit(solution)/shard_map/ppermute | solution.py:284
  15.0 47.8 %collective-permute-start.11 = (f32[264,256]{1,0:T(8,128)}, f32[264,256]{1,0:T(8,128)}, u32[]{:S(2)}, u32[]{:S(2)}) collective-permute-start(f32[264,256]{1,0:T(8,128)} %pad_maximum_fusion.4), channel_id=1, source_target_pairs={{8,0},{16,8},{24,16},{9,1},{17,9},{25,17},{10,2},{18,10},{26,18},{... | collective-permute-start | bytes 811016 | tf_op jit(solution)/shard_map/ppermute | solution.py:284
  19.0 7.1 %collective-permute-start.1 = (f32[192,256]{1,0:T(8,128)S(1)}, f32[192,256]{1,0:T(8,128)S(1)}, u32[]{:S(2)}, u32[]{:S(2)}) collective-permute-start(f32[192,256]{1,0:T(8,128)S(1)} %get-tuple-element.33), channel_id=1, source_target_pairs={{0,2},{1,3},{2,0},{3,1},{4,6},{5,7},{6,4},{7,5},{8,10},{9,11},{10,... | collective-permute-start | bytes 589832 | tf_op jit(solution)/shard_map/ppermute | solution.py:21
  20.6 9.3 %collective-permute-start.5 = (f32[192,256]{1,0:T(8,128)S(1)}, f32[192,256]{1,0:T(8,128)S(1)}, u32[]{:S(2)}, u32[]{:S(2)}) collective-permute-start(f32[192,256]{1,0:T(8,128)S(1)} %get-tuple-element.34), channel_id=1, source_target_pairs={{0,8},{8,0},{16,24},{24,16},{1,9},{9,1},{17,25},{25,17},{2,10},{10... | collective-permute-start | bytes 589832 | tf_op jit(solution)/shard_map/ppermute | solution.py:21
  30.0 6.2 %collective-permute-start.2 = (f32[192,256]{1,0:T(8,128)S(1)}, f32[192,256]{1,0:T(8,128)S(1)}, u32[]{:S(2)}, u32[]{:S(2)}) collective-permute-start(f32[192,256]{1,0:T(8,128)S(1)} %get-tuple-element.31), channel_id=1, source_target_pairs={{0,4},{1,5},{2,6},{3,7},{4,0},{5,1},{6,2},{7,3},{8,12},{9,13},{10,... | collective-permute-start | bytes 589832 | tf_op jit(solution)/shard_map/ppermute | solution.py:21
  31.5 10.1 %collective-permute-start.6 = (f32[192,256]{1,0:T(8,128)S(1)}, f32[192,256]{1,0:T(8,128)S(1)}, u32[]{:S(2)}, u32[]{:S(2)}) collective-permute-start(f32[192,256]{1,0:T(8,128)S(1)} %get-tuple-element.32), channel_id=1, source_target_pairs={{0,16},{8,24},{16,0},{24,8},{1,17},{9,25},{17,1},{25,9},{2,18},{10... | collective-permute-start | bytes 589832 | tf_op jit(solution)/shard_map/ppermute | solution.py:21
  36.2 9.5 %collective-permute-start.3 = (f32[192,256]{1,0:T(8,128)S(1)}, f32[192,256]{1,0:T(8,128)S(1)}, u32[]{:S(2)}, u32[]{:S(2)}) collective-permute-start(f32[192,256]{1,0:T(8,128)S(1)} %add.209), channel_id=1, source_target_pairs={{0,8},{8,0},{16,24},{24,16},{1,9},{9,1},{17,25},{25,17},{2,10},{10... | collective-permute-start | bytes 589832 | tf_op jit(solution)/shard_map/ppermute | solution.py:21
  41.6 6.8 %collective-permute-start.7 = (f32[192,256]{1,0:T(8,128)S(1)}, f32[192,256]{1,0:T(8,128)S(1)}, u32[]{:S(2)}, u32[]{:S(2)}) collective-permute-start(f32[192,256]{1,0:T(8,128)S(1)} %add.213), channel_id=1, source_target_pairs={{0,2},{1,3},{2,0},{3,1},{4,6},{5,7},{6,4},{7,5},{8,10},{9,11},{10,... | collective-permute-start | bytes 589832 | tf_op jit(solution)/shard_map/ppermute | solution.py:21
  45.7 10.9 %collective-permute-start.4 = (f32[192,256]{1,0:T(8,128)S(1)}, f32[192,256]{1,0:T(8,128)S(1)}, u32[]{:S(2)}, u32[]{:S(2)}) collective-permute-start(f32[192,256]{1,0:T(8,128)S(1)} %add.210), channel_id=1, source_target_pairs={{0,16},{8,24},{16,0},{24,8},{1,17},{9,25},{17,1},{25,9},{2,18},{10... | collective-permute-start | bytes 589832 | tf_op jit(solution)/shard_map/ppermute | solution.py:21
  48.5 8.2 %collective-permute-start.8 = (f32[192,256]{1,0:T(8,128)S(1)}, f32[192,256]{1,0:T(8,128)S(1)}, u32[]{:S(2)}, u32[]{:S(2)}) collective-permute-start(f32[192,256]{1,0:T(8,128)S(1)} %add.214), channel_id=1, source_target_pairs={{0,4},{1,5},{2,6},{3,7},{4,0},{5,1},{6,2},{7,3},{8,12},{9,13},{10,... | collective-permute-start | bytes 589832 | tf_op jit(solution)/shard_map/ppermute | solution.py:21
  56.6 0.7 copy-start.2
  57.3 0.8 copy-start.3
  58.1 11.0 %collective-permute-start.9 = (f32[384,256]{1,0:T(8,128)}, f32[384,256]{1,0:T(8,128)}, u32[]{:S(2)}, u32[]{:S(2)}) collective-permute-start(f32[384,256]{1,0:T(8,128)} %pad_maximum_fusion.2), channel_id=1, source_target_pairs={{0,1},{1,0},{2,3},{3,2},{4,5},{5,4},{6,7},{7,6},{8,9},{9,8},{10,11... | collective-permute-start | bytes 1179656 | tf_op jit(solution)/shard_map/ppermute | solution.py:21
  67.0 4.6 %copy-start = (f32[32,2,8,256]{3,2,1,0:T(8,128)S(1)}, f32[32,2,8,256]{3,2,1,0:T(8,128)}, u32[]{:S(2)}) copy-start(f32[32,2,8,256]{3,2,1,0:T(8,128)} %get-tuple-element.24) | copy-start | bytes 1572868
  68.1 3.5 %copy-start.4 = (f32[256,256]{1,0:T(8,128)}, f32[256,256]{1,0:T(8,128)S(1)}, u32[]{:S(2)}) copy-start(f32[256,256]{1,0:T(8,128)S(1)} %slice.204) | copy-start | bytes 786436
  69.2 2.5 %copy-start.5 = (f32[256,256]{1,0:T(8,128)}, f32[256,256]{1,0:T(8,128)S(1)}, u32[]{:S(2)}) copy-start(f32[256,256]{1,0:T(8,128)S(1)} %slice.206) | copy-start | bytes 786436
  72.7 57.8 %collective-permute-start.12 = (f32[584,256]{1,0:T(8,128)}, f32[584,256]{1,0:T(8,128)}, u32[]{:S(2)}, u32[]{:S(2)}) collective-permute-start(f32[584,256]{1,0:T(8,128)} %pad_maximum_fusion), channel_id=1, source_target_pairs={{0,1},{1,2},{2,3},{3,4},{4,5},{5,6},{6,7},{7,0},{8,9},{9,10},{10,1... | collective-permute-start | bytes 1794056 | tf_op jit(solution)/shard_map/ppermute | solution.py:284
  73.2 1.8 copy-start.13
  75.0 5.4 %copy-start.6 = (f32[3,256,256]{2,1,0:T(8,128)S(1)}, f32[3,256,256]{2,1,0:T(8,128)}, u32[]{:S(2)}) copy-start(f32[3,256,256]{2,1,0:T(8,128)} %param.12) | copy-start | bytes 2359300
  75.0 5.4 %copy-start.15 = (f32[3,256]{1,0:T(4,128)S(1)}, f32[3,256]{1,0:T(4,128)}, u32[]{:S(2)}) copy-start(f32[3,256]{1,0:T(4,128)} %param.11) | copy-start | bytes 9220
  75.9 55.5 %collective-permute-start.13 = (f32[584,256]{1,0:T(8,128)S(1)}, f32[584,256]{1,0:T(8,128)S(1)}, u32[]{:S(2)}, u32[]{:S(2)}) collective-permute-start(f32[584,256]{1,0:T(8,128)S(1)} %pad_maximum_fusion.1), channel_id=1, source_target_pairs={{1,0},{2,1},{3,2},{4,3},{5,4},{6,5},{7,6},{0,7},{9,8},{10,9},{11,1... | collective-permute-start | bytes 1794056 | tf_op jit(solution)/shard_map/ppermute | solution.py:284
  78.2 53.3 %copy-start.1 = (f32[3,1,16,8]{1,3,2,0:T(8,128)S(1)}, f32[3,1,16,8]{1,3,2,0:T(8,128)}, u32[]{:S(2)}) copy-start(f32[3,1,16,8]{1,3,2,0:T(8,128)} %copy.13) | copy-start | bytes 4612
  78.2 53.3 %copy-start.9 = (f32[32,16,8]{0,2,1:T(8,128)S(1)}, f32[32,16,8]{0,2,1:T(8,128)}, u32[]{:S(2)}) copy-start(f32[32,16,8]{0,2,1:T(8,128)} %param.18) | copy-start | bytes 49156
  78.2 53.3 %copy-start.11 = (f32[32,16,8]{0,2,1:T(8,128)S(1)}, f32[32,16,8]{0,2,1:T(8,128)}, u32[]{:S(2)}) copy-start(f32[32,16,8]{0,2,1:T(8,128)} %param.17) | copy-start | bytes 49156

commit v2 on v1

v2 whole, which is shorter than its diff:
```python
import functools

import jax
import jax.numpy as jnp
from jax import lax
from jax.experimental import pallas as pl
from jax.experimental.pallas import tpu as pltpu
from jax.sharding import PartitionSpec as P

NBATCH = 3
CLAT = 32
CLON = 16
HALO = 2
LANES = 128
F32 = jnp.float32
BF16 = jnp.bfloat16
VMEM = pl.BlockSpec(memory_space=pltpu.VMEM)


def shifted(x, axis, flip):
    size = lax.axis_size(axis)
    return lax.ppermute(x, axis, [(i, i ^ flip) for i in range(size)])


def stages(axis, first):
    size, out = lax.axis_size(axis), []
    while first < size:
        out.append((axis, first))
        first *= 2
    return out


def gather_kernel(cells, tiles, spot, state_hbm, first_ref, second_ref, state_ref, sem):
    count, half, members = first_ref.shape
    core = lax.rem(spot[1], 2)

    def owned(b):
        return jnp.logical_and(tiles[b, 0] == spot[0], tiles[b, 1] == spot[1])

    any_owned = owned(0)
    for b in range(1, count):
        any_owned = jnp.logical_or(any_owned, owned(b))

    @pl.when(any_owned)
    def _():
        copy = pltpu.make_async_copy(state_hbm, state_ref, sem)
        copy.start()
        copy.wait()

    for b in range(count):
        mine = owned(b)
        for side, ref in enumerate((first_ref, second_ref)):
            start = lax.rem(core + side, 2) * half

            @pl.when(mine)
            def _():
                @pl.loop(0, half // 8)
                def _(i):
                    for n in range(8):
                        row = state_ref[pl.ds(cells[b, start + i * 8 + n], 1), :]
                        ref[b, pl.ds(i * 8 + n, 1), :] = row

            @pl.when(jnp.logical_not(mine))
            def _():
                ref[b] = jnp.zeros((half, members), F32)


def gather(ensemble, cells, tiles, spot):
    members = ensemble.shape[-1]
    flat = ensemble.reshape(-1, members)
    count, nobs = cells.shape
    smem = pl.BlockSpec(memory_space=pltpu.SMEM)
    out = jax.ShapeDtypeStruct((count, nobs // 2, members), F32)
    return pl.pallas_call(
        gather_kernel,
        out_shape=[out, out],
        in_specs=[smem] * 3 + [pl.BlockSpec(memory_space=pl.ANY)],
        out_specs=[VMEM] * 2,
        scratch_shapes=[pltpu.VMEM(flat.shape, F32), pltpu.SemaphoreType.DMA],
        compiler_params=pltpu.CompilerParams(vmem_limit_bytes=24 << 20),
    )(cells, tiles, spot, flat)


def spread_out(mine, half, fillers):
    fillers, made = list(fillers), []
    a, b = mine[:, :half], mine[:, half:]
    lon, lat = stages("lon", 2), stages("lat", 1)
    for (a_axis, a_flip), (b_axis, b_flip) in zip(lon + lat, lat + lon):
        a_moved, b_moved = shifted(a, a_axis, a_flip), shifted(b, b_axis, b_flip)
        a, b = a + a_moved, b + b_moved
        if fillers:
            a, b, filler = lax.optimization_barrier((a, b, fillers.pop(0)))
            made.append(filler)
    return (a, b, shifted(a, "lon", 1), shifted(b, "lon", 1)), made + fillers


def taper(lat_a, lon_a, lat_b, lon_b, radius, total_lon):
    lat_gap = (lat_a[:, None] - lat_b[None, :]).astype(F32)
    lon_gap = jnp.abs(lon_a[:, None] - lon_b[None, :])
    lon_gap = jnp.minimum(lon_gap, total_lon - lon_gap).astype(F32)
    radius = radius.astype(F32)
    ratio = 1.0 - (jnp.square(lat_gap) + jnp.square(lon_gap)) / (radius * radius)
    return jnp.square(jnp.maximum(ratio, 0.0))


def split(x):
    high = x.astype(BF16)
    return high, (x - high.astype(F32)).astype(BF16)


def exact_dot(a, b):
    return jnp.dot(a, b, precision=lax.Precision.HIGHEST, preferred_element_type=F32)


def split_dot(a, b_high, *b_rest):
    high, low = split(a)
    dot = functools.partial(jnp.dot, preferred_element_type=F32)
    total = dot(high, b_high) + dot(low, b_high)
    for b in b_rest:
        total = total + dot(high, b)
    return total


def lane_spread(x, lane):
    return jnp.take_along_axis(x, jnp.full(x.shape, lane, jnp.int32), axis=1)


def panel(strips):
    strips, shape = list(strips), strips[0].shape
    lane = lax.broadcasted_iota(jnp.int32, shape, 1)
    row = lax.broadcasted_iota(jnp.int32, shape, 0)
    for g, first in enumerate(strips):
        at = 8 * g
        block = jnp.logical_and(lane >= at, lane < at + 8)
        first = strips[g]
        diag = [lane_spread(first, at + c) for c in range(8)]
        left = {
            h: [lane_spread(strip, at + c) for c in range(8)]
            for h, strip in enumerate(strips)
            if h != g
        }
        scaled = jnp.where(block, jnp.where(lane == row + at, 1.0, 0.0), first)
        for k in range(0, 8, 2):

            def pick(x, n):
                return jnp.broadcast_to(x[n : n + 1], shape)

            p, q, r = pick(diag[k], k), pick(diag[k], k + 1), pick(diag[k + 1], k + 1)
            pivot = 1.0 / (p * r - q * q)

            def reduced(x):
                upper, lower = pick(x, k), pick(x, k + 1)
                upper, lower = (r * upper - q * lower) * pivot, (p * lower - q * upper) * pivot
                x = x - (diag[k] * upper + diag[k + 1] * lower)
                return jnp.where(row == k, upper, jnp.where(row == k + 1, lower, x))

            diag[k + 2 :] = [reduced(x) for x in diag[k + 2 :]]
            scaled = reduced(scaled)
        rows = [jnp.broadcast_to(scaled[c : c + 1], shape) for c in range(8)]
        for h, columns in left.items():
            terms = [columns[c] * rows[c] for c in range(8)]
            while len(terms) > 1:
                terms = [terms[j] + terms[j + 1] for j in range(0, len(terms), 2)]
            strips[h] = jnp.where(block, 0.0, strips[h]) - terms[0]
        strips[g] = scaled
    return strips


def inverse(a, block=64):
    size = a.shape[0]

    def turn(_, a):
        top = panel([a[8 * i : 8 * i + 8] for i in range(block // 8)])
        top, rest = jnp.concatenate(top), a[block:]
        lane = lax.broadcasted_iota(jnp.int32, rest.shape, 1)
        rest = jnp.where(lane < block, 0.0, rest) - exact_dot(rest[:, :block], top)
        return pltpu.roll(jnp.concatenate([rest, top]), size - block, 1)

    return lax.fori_loop(0, size // block, turn, a)


def solve_kernel(*refs):
    pieces, refs = refs[:4], refs[4:]
    target_ref, var_ref, mutual_ref, out_hbm, y_ref, out_ref, sem = refs
    count, nobs, members = target_ref.shape
    half = nobs // 2
    for n, piece in enumerate(pieces):
        size = piece.shape[1]
        y_ref[:, n * size : (n + 1) * size] = piece[...]
    diagonal = lax.broadcasted_iota(jnp.int32, (nobs, nobs), 0) == lax.broadcasted_iota(
        jnp.int32, (nobs, nobs), 1
    )

    @pl.loop(0, count)
    def _(b):
        y = y_ref[b]
        spread = y - jnp.sum(y, axis=1, keepdims=True) / members
        spread_t = spread.T
        out_ref[b, 0], out_ref[b, 1] = split(spread_t)
        cov = exact_dot(spread, spread_t) / (members - 1)
        cov = cov + jnp.where(diagonal, jnp.broadcast_to(var_ref[b], (nobs, nobs)), 0.0)
        right = target_ref[b] - y
        lower = cov[half:, :half]
        upper = jnp.concatenate([cov[:half, half:], right[:half]], axis=1)
        upper = exact_dot(inverse(cov[:half, :half]), upper)
        rest = exact_dot(lower, upper)
        schur = inverse(cov[half:, half:] - rest[:, :half])
        w_second = exact_dot(schur, right[half:] - rest[:, half:])
        w_first = upper[:, half:] - exact_dot(upper[:, :half], w_second)
        w = jnp.concatenate([w_first, w_second], axis=0)
        high, mid = split(w)
        out_ref[b, 2] = high
        out_ref[b, 3] = mid
        out_ref[b, 4] = (w - high.astype(F32) - mid.astype(F32)).astype(BF16)
        pltpu.make_async_copy(out_ref.at[b], out_hbm.at[b], sem).start()

        @pl.loop(b + 1, count)
        def _(later):
            y_later = y_ref[later]
            gain = exact_dot(y_later, spread_t) * mutual_ref[b + later - 1]
            y_ref[later] = y_later + exact_dot(gain, w)

    pltpu.make_async_copy(out_ref, out_hbm, sem).wait()


def solve(pieces, target, variance, mutual):
    count, nobs, members = target.shape
    out = (count, 5, nobs, members)
    return pl.pallas_call(
        solve_kernel,
        out_shape=jax.ShapeDtypeStruct(out, BF16),
        in_specs=[VMEM] * 7,
        out_specs=pl.BlockSpec(memory_space=pl.ANY),
        scratch_shapes=[
            pltpu.VMEM((count, nobs, members), F32),
            pltpu.VMEM(out, BF16),
            pltpu.SemaphoreType.DMA,
        ],
        compiler_params=pltpu.CompilerParams(vmem_limit_bytes=40 << 20),
        cost_estimate=pl.CostEstimate(
            flops=60 * count * nobs**3, bytes_accessed=4 * 8 * target.size, transcendentals=0
        ),
    )(*pieces, target, variance[:, None, :], mutual)


def sweep(source, j, height, coef_at, store):
    middle = [source[i, j + 1] for i in range(height + 2)]
    for i in range(height):
        near = (middle[i + 1], middle[i], middle[i + 2], source[i + 1, j], source[i + 1, j + 2])
        total = None
        for coef, part in zip(coef_at(i), near):
            coef = jnp.concatenate([coef] * (part.shape[-1] // coef.shape[-1]), axis=-1)
            total = part * coef if total is None else total + part * coef
        store(i, total)


def five(lat_speed, lon_speed, rate):
    return (
        1.0 - jnp.abs(lat_speed) - jnp.abs(lon_speed) - 4.0 * rate,
        jnp.maximum(lat_speed, 0.0) + rate,
        rate - jnp.minimum(lat_speed, 0.0),
        jnp.maximum(lon_speed, 0.0) + rate,
        rate - jnp.minimum(lon_speed, 0.0),
    )


def move_kernel(chunk, *refs):
    pieces, refs = refs[:5], refs[5:]
    taper_hbm, coef_hbm, factor_hbm, out_hbm, x_ref, taper_ref, factor_ref = refs[:7]
    coef_ref, wide_ref, z_ref, out_ref, sems, out_sem = refs[7:]
    count = factor_ref.shape[0]
    tall, wide, levels, members = x_ref.shape
    inner = (pl.ds(HALO, tall - 2 * HALO), pl.ds(HALO, wide - 2 * HALO))
    places = (
        inner,
        (pl.ds(0, HALO), inner[1]),
        (pl.ds(tall - HALO, HALO), inner[1]),
        (slice(None), pl.ds(0, HALO)),
        (slice(None), pl.ds(wide - HALO, HALO)),
    )
    heights = (tall - 2 * HALO, HALO, HALO, tall, tall)
    copies = [
        pltpu.make_async_copy(piece.at[pl.ds(0, height)], x_ref.at[place], sems.at[n])
        for n, (piece, place, height) in enumerate(zip(pieces, places, heights))
    ]
    copies.append(pltpu.make_async_copy(taper_hbm, taper_ref, sems.at[5]))
    copies.append(pltpu.make_async_copy(factor_hbm, factor_ref, sems.at[13]))
    coef_copies = [
        pltpu.make_async_copy(coef_hbm, coef_ref.at[:, pl.ds(1, wide - 4)], sems.at[6])
    ]
    for n in range(3):
        for side in range(2):
            source = pieces[3 + side].at[tall + n // 2, n % 2, :, pl.ds(0, coef_ref.shape[-1])]
            to = coef_ref.at[n, side * (wide - 3)]
            coef_copies.append(pltpu.make_async_copy(source, to, sems.at[7 + 2 * n + side]))
    for copy in copies + coef_copies:
        copy.start()
    for copy in copies:
        copy.wait()

    @pl.loop(0, tall // chunk)
    def _(i):
        at = pl.ds(i * chunk, chunk)
        x = x_ref[at].reshape(chunk * wide * levels, members)
        for b in range(count):
            gain = split_dot(x, factor_ref[b, 0], factor_ref[b, 1])
            gain = gain.reshape(chunk * wide, levels, -1)
            gain = gain * taper_ref[b, at].reshape(chunk * wide, -1)[:, None, :]
            gain = gain.reshape(chunk * wide * levels, -1)
            x = x + split_dot(gain, factor_ref[b, 2], factor_ref[b, 3], factor_ref[b, 4])
        x_ref[at] = x.reshape(chunk, wide, levels, members)

    for copy in coef_copies:
        copy.wait()

    @pl.loop(0, wide - 2)
    def _(j):
        tiles = five(*[coef_ref[n, j] for n in range(3)])

        def coef_at(i):
            found = [jnp.broadcast_to(tile[:, i : i + 1], (levels, LANES)) for tile in tiles]
            for n, coef in enumerate(found):
                wide_ref[n, i, j] = coef
            return found

        def store(i, value):
            z_ref[i, j] = value

        sweep(x_ref, j, tall - 2, coef_at, store)

    @pl.loop(0, wide - 4)
    def _(j):
        def store(i, value):
            out_ref[i, j] = value

        def coef_at(i):
            return [wide_ref[n, i + 1, j + 1] for n in range(5)]

        sweep(z_ref, j, tall - 4, coef_at, store)
        pltpu.make_async_copy(out_ref.at[:, j], out_hbm.at[:, j], out_sem).start()

    pltpu.make_async_copy(out_ref, out_hbm, out_sem).wait()


def move(pieces, tapers, coefs, factors):
    tall, wide = pieces[0].shape[0] + 2 * HALO, pieces[0].shape[1] + 2 * HALO
    levels, members = pieces[0].shape[2:]
    hbm = pl.BlockSpec(memory_space=pl.ANY)
    return pl.pallas_call(
        functools.partial(move_kernel, 12 if tall % 12 == 0 else 1),
        out_shape=jax.ShapeDtypeStruct(pieces[0].shape, F32),
        in_specs=[hbm] * 8,
        out_specs=hbm,
        scratch_shapes=[
            pltpu.VMEM((tall, wide, levels, members), F32),
            pltpu.VMEM(tapers.shape, F32),
            pltpu.VMEM(factors.shape, BF16),
            pltpu.VMEM((3, wide - 2, levels, coefs.shape[-1]), F32),
            pltpu.VMEM((5, tall - 2, wide - 2, levels, LANES), F32),
            pltpu.VMEM((tall - 2, wide - 2, levels, members), F32),
            pltpu.VMEM(pieces[0].shape, F32),
            pltpu.SemaphoreType.DMA((14,)),
            pltpu.SemaphoreType.DMA,
        ],
        compiler_params=pltpu.CompilerParams(vmem_limit_bytes=60 << 20),
    )(*pieces, tapers, coefs, factors)


def lanes(x, count):
    return jnp.pad(x, [(0, 0)] * (x.ndim - 1) + [(0, count - x.shape[-1])])


def neighbours(before, after, axis, wrap):
    size = lax.axis_size(axis)
    up = [(i, (i + 1) % size) for i in range(size if wrap else size - 1)]
    down = [(j, i) for i, j in up]
    return lax.ppermute(before, axis, up), lax.ppermute(after, axis, down)


def shards(
    ensemble,
    obs_values,
    obs_noise,
    obs_var,
    obs_cells,
    owner_tiles,
    radius,
    courant_lat,
    courant_lon,
    diffusivity,
):
    lat_index = lax.axis_index("lat")
    lon_index = lax.axis_index("lon")
    total_lon = CLON * lax.axis_size("lon")
    levels, members = ensemble.shape[2:]
    nobs = obs_cells.shape[1]

    core = lon_index % 2
    half = nobs // 2
    spot = jnp.stack([lat_index, lon_index])
    mine, others = gather(ensemble, obs_cells, owner_tiles, spot)
    mine = mine + shifted(others, "lon", 1)
    (
        mine,
        obs_cells,
        obs_values,
        obs_var,
        obs_noise,
        owner_tiles,
        radius,
        courant_lat,
        courant_lon,
        diffusivity,
        south,
        north,
    ) = lax.optimization_barrier(
        (
            mine,
            obs_cells,
            obs_values,
            obs_var,
            obs_noise,
            owner_tiles,
            radius,
            courant_lat,
            courant_lon,
            diffusivity,
            ensemble[-HALO:],
            ensemble[:HALO],
        )
    )

    def own_first(x):
        x = jnp.concatenate([x, x[:, :half]], axis=1)
        return lax.dynamic_slice_in_dim(x, core * half, nobs, 1)

    obs_cells, obs_values, obs_var, obs_noise = map(
        own_first, (obs_cells, obs_values, obs_var, obs_noise)
    )

    speeds = jnp.stack([courant_lat, courant_lon, diffusivity]).transpose(0, 2, 3, 1)
    thin = lanes(speeds[..., -1:].transpose(3, 1, 2, 0), members)
    south = jnp.concatenate([south, thin])
    thin = lanes(speeds[..., :1].transpose(3, 1, 2, 0), members)
    north = jnp.concatenate([north, thin])
    south, north = neighbours(south, north, "lat", False)
    south_thin, north_thin = (
        side[HALO:, :, :, :3].transpose(3, 1, 2, 0) for side in (south, north)
    )
    speeds = jnp.concatenate([south_thin, speeds, north_thin], axis=-1)
    speeds = lanes(speeds, LANES)

    tall, wide = ensemble.shape[0] + 2 * HALO, ensemble.shape[1] + 2 * HALO
    place = obs_cells // levels
    obs_lat = owner_tiles[:, :1] * CLAT + place // CLON
    obs_lon = owner_tiles[:, 1:] * CLON + place % CLON
    lat_cells = lat_index * CLAT - HALO + jnp.arange(tall, dtype=jnp.int32)
    lon_cells = lon_index * CLON - HALO + jnp.arange(wide, dtype=jnp.int32)
    lon_cells = (lon_cells + total_lon) % total_lon
    lat_cells = jnp.broadcast_to(lat_cells[:, None], (tall, wide)).reshape(-1)
    lon_cells = jnp.broadcast_to(lon_cells[None, :], (tall, wide)).reshape(-1)
    tapers = jnp.stack(
        [
            taper(lat_cells, lon_cells, obs_lat[b], obs_lon[b], radius[b], total_lon)
            for b in range(NBATCH)
        ]
    ).reshape(NBATCH, tall, wide, nobs) / (members - 1)
    mutual = jnp.stack(
        [
            taper(obs_lat[c], obs_lon[c], obs_lat[b], obs_lon[b], radius[b], total_lon)
            for b, c in ((0, 1), (0, 2), (1, 2))
        ]
    ) / (members - 1)
    target = obs_values[:, :, None] + jnp.sqrt(obs_var)[:, :, None] * obs_noise

    def side(at, extent, lane):
        edge = jnp.concatenate([part[:, at:extent] for part in (south[:HALO], ensemble, north[:HALO])])
        tile = lanes(speeds[:, lane], members)
        tile = jnp.pad(tile, ((0, 1), (0, 0), (0, 0))).reshape((2, 2) + tile.shape[1:])
        return jnp.concatenate([edge, tile])

    last = ensemble.shape[1]
    before, after = side(last - HALO, last, last - 1), side(0, HALO, 0)
    pieces, (tapers, (target, mutual), (speeds, before, after)) = spread_out(
        mine, half // 2, (tapers, (target, mutual), (speeds, before, after))
    )
    pieces, before, after = lax.optimization_barrier((pieces, before, after))
    west, east = neighbours(before, after, "lon", True)
    factors = solve(pieces, target, obs_var, mutual)
    cells = (ensemble, south, north, west, east)
    return move(cells, tapers, speeds, factors)


def solution(mesh):
    cells = P("lat", "lon", None)
    in_specs = (P("lat", "lon", None, None),) + (P(),) * 6 + (cells,) * 3
    out_specs = P("lat", "lon", None, None)
    return jax.shard_map(
        shards, mesh=mesh, in_specs=in_specs, out_specs=out_specs, check_vma=False
    )
```

time: 181 us -> 131 us (0.72)
  Pallas kernels: 87.8 us -> 64.2 us
  local copies, waits for them, and re-layouts: 28.1 us -> 16.4 us
  waiting for transfers between devices: 26.7 us -> 17.4 us
  other arithmetic: 15.3 us -> 7.64 us
  starting transfers between devices: 19.9 us -> 22.1 us
    pallas_call x2 -> x3, Pallas kernels: 87.8 us -> 64.2 us  [the longest x1 37.4 us: move(): pl.pallas_call(functools.partial(move_kernel, 12 if tall % 12 == 0 else 1...]
    ppermute x10 -> x11, waiting for transfers between devices: 26.7 us -> 16.5 us  [shifted(): return lax.ppermute(x, axis, [(i, i ^ flip) for i in range(size)])]
    unnamed x39 -> x37, local copies, waits for them, and re-layouts: 2.11 us -> 11.7 us
    slice x22 -> x16, local copies, waits for them, and re-layouts: 13 us -> 3.86 us  [the longest x3 2.92 us: side(): part[:, at:extent]]
    broadcast_in_dim x3 -> x0, local copies, waits for them, and re-layouts: 5.73 us -> none  [the longest x1 5.64 us: shards(): coefs = jnp.broadcast_to(coefs[..., None], coefs.shape + (128,))]
    ppermute x10 -> x11, starting transfers between devices: 10.5 us -> 15.6 us  [shifted(): return lax.ppermute(x, axis, [(i, i ^ flip) for i in range(size)])]
    gather x1 -> x0, local copies, waits for them, and re-layouts: 4.34 us -> none  [shards(): rows = ensemble.reshape(-1, members)[obs_cells.reshape(-1)]]
    ppermute x4, starting transfers between devices: 9.37 us -> 6.43 us  [neighbours(): return (lax.ppermute(before, axis, up), lax.ppermute(after, axis, down))]
  transfers between devices with their start and end apart: 14 -> 15, of which waited for: 7 -> 7; matrix products, arithmetic and copies ran while one was open for 13% -> 10% of each run, Pallas kernels for 27% -> 20%
where the time goes in v2:
time: 131 us; the launch traced here: 130 us
  Pallas kernels  64.2 us (49%)
  starting transfers between devices  22.1 us (17%)
  waiting for transfers between devices  17.4 us (13%)
  local copies, waits for them, and re-layouts  16.4 us (13%)
  other arithmetic  7.64 us (6%)
  between operations  2.59 us (2%)
    pallas_call x1, Pallas kernels, move(): pl.pallas_call(functools.partial(move_kernel, 12 if tall % 12 == 0 else 1...  37.4 us
    pallas_call x1, Pallas kernels, solve(): pl.pallas_call(solve_kernel, out_shape=jax.ShapeDtypeStruct(out, BF16), i...  26.1 us
    ppermute x11, waiting for transfers between devices, shifted(): return lax.ppermute(x, axis, [(i, i ^ flip) for i in range(size)])  16.5 us
    ppermute x11, starting transfers between devices, shifted(): return lax.ppermute(x, axis, [(i, i ^ flip) for i in range(size)])  15.6 us
    unnamed x37, local copies, waits for them, and re-layouts  11.7 us
    ppermute x4, starting transfers between devices, neighbours(): return (lax.ppermute(before, axis, up), lax.ppermute(after, axis, down))  6.43 us
    slice x3, local copies, waits for them, and re-layouts, side(): part[:, at:extent]  2.92 us
  transfers between devices with their start and end apart: 15, of which 7 were waited for; matrix products, arithmetic and copies ran while one was open for 10% of the time, Pallas kernels for 20%

profile of v2, /device:TPU:0, one launch (start us, length us, event | category | flops | bytes accessed | tf_op | source)
XLA Modules:
  0.0 130.3 jit_solution(11129908708708639642)
XLA Ops:
  0.8 2.2 %copy-done = f32[32,16,8,256]{3,2,1,0:T(8,128)S(1)} copy-done((f32[32,16,8,256]{3,2,1,0:T(8,128)S(1)}, f32[32,16,8,256]{3,2,1,0:T(8,128)}, u32[]{:S(2)}) %copy-start) | copy-done | bytes 4194328
  5.2 1.3 fusion.56
  9.6 0.9 copy.28
  10.5 0.9 copy.27
  11.4 3.0 %collective-permute-start.4 = (f32[3,64,256]{2,1,0:T(8,128)S(1)}, f32[3,64,256]{2,1,0:T(8,128)S(1)}, u32[]{:S(2)}, u32[]{:S(2)}) collective-permute-start(f32[3,64,256]{2,1,0:T(8,128)S(1)} %get-tuple-element.83), channel_id=1, source_target_pairs={{0,8},{8,0},{16,24},{24,16},{1,9},{9,1},{17,25},{25,17},{2,10},{10... | collective-permute-start | bytes 589832 | tf_op jit(solution)/shard_map/ppermute | solution.py:22
  14.3 1.5 %collective-permute-start.3 = (f32[3,64,256]{2,1,0:T(8,128)S(1)}, f32[3,64,256]{2,1,0:T(8,128)S(1)}, u32[]{:S(2)}, u32[]{:S(2)}) collective-permute-start(f32[3,64,256]{2,1,0:T(8,128)S(1)} %get-tuple-element.84), channel_id=1, source_target_pairs={{0,2},{1,3},{2,0},{3,1},{4,6},{5,7},{6,4},{7,5},{8,10},{9,11},{10,... | collective-permute-start | bytes 589832 | tf_op jit(solution)/shard_map/ppermute | solution.py:22
  15.9 2.4 %collective-permute-start.1 = (f32[3,16,8,256]{3,2,1,0:T(8,128)S(1)}, f32[3,16,8,256]{3,2,1,0:T(8,128)S(1)}, u32[]{:S(2)}, u32[]{:S(2)}) collective-permute-start(f32[3,16,8,256]{3,2,1,0:T(8,128)S(1)} %select_maximum_fusion.1), channel_id=1, source_target_pairs={{0,8},{8,16},{16,24},{1,9},{9,17},{17,25},{2,10},{10,18},{18,26},{... | collective-permute-start | bytes 1179656 | tf_op jit(solution)/shard_map/ppermute | solution.py:377
  19.0 1.4 %collective-permute-start.2 = (f32[3,16,8,256]{3,2,1,0:T(8,128)}, f32[3,16,8,256]{3,2,1,0:T(8,128)}, u32[]{:S(2)}, u32[]{:S(2)}) collective-permute-start(f32[3,16,8,256]{3,2,1,0:T(8,128)} %select_maximum_fusion), channel_id=1, source_target_pairs={{8,0},{16,8},{24,16},{9,1},{17,9},{25,17},{10,2},{18,10},{26,18},{... | collective-permute-start | bytes 1179656 | tf_op jit(solution)/shard_map/ppermute | solution.py:377
  21.7 1.7 %maximum_multiply_fusion.refs_5_ = f32[3,36,20,256]{3,2,1,0:T(8,128)} fusion(f32[1,36,20,256]{3,2,1,0:T(8,128)S(1)} %get-tuple-element.100, f32[1,36,20,256]{3,2,1,0:T(8,128)S(1)} %get-tuple-element.99, f32[1,36,20,256]{3,2,1,0:T(8,128)S(1)} %get-tuple-element.98), kind=kLoop, calls=%fused_computation | loop fusion | flops 1658880 | bytes 4423680 | tf_op jit(solution)/shard_map/div | solution.py:462
  23.6 3.9 %collective-permute-start.5 = (f32[3,64,256]{2,1,0:T(8,128)S(1)}, f32[3,64,256]{2,1,0:T(8,128)}, u32[]{:S(2)}, u32[]{:S(2)}) collective-permute-start(f32[3,64,256]{2,1,0:T(8,128)S(1)} %get-tuple-element.48), channel_id=1, source_target_pairs={{0,4},{1,5},{2,6},{3,7},{4,0},{5,1},{6,2},{7,3},{8,12},{9,13},{10,... | collective-permute-start | bytes 589832 | tf_op jit(solution)/shard_map/ppermute | solution.py:22
  27.4 2.5 %collective-permute-start.6 = (f32[3,64,256]{2,1,0:T(8,128)S(1)}, f32[3,64,256]{2,1,0:T(8,128)}, u32[]{:S(2)}, u32[]{:S(2)}) collective-permute-start(f32[3,64,256]{2,1,0:T(8,128)S(1)} %get-tuple-element.49), channel_id=1, source_target_pairs={{0,16},{8,24},{16,0},{24,8},{1,17},{9,25},{17,1},{25,9},{2,18},{10... | collective-permute-start | bytes 589832 | tf_op jit(solution)/shard_map/ppermute | solution.py:22
  31.0 0.9 copy.25
  31.9 0.9 collective-permute-done.2.refs_2_
  32.8 0.8 slice.174
  33.6 1.6 %copy.26 = f32[1,16,8,3]{0,2,1,3:T(8,128)} copy(f32[1,16,8,3]{3,2,1,0:T(8,128)S(1)} %slice.174) | data formatting | bytes 3072
  35.2 1.0 add.210
  36.2 6.1 %collective-permute-done.6 = f32[3,64,256]{2,1,0:T(8,128)} collective-permute-done((f32[3,64,256]{2,1,0:T(8,128)S(1)}, f32[3,64,256]{2,1,0:T(8,128)}, u32[]{:S(2)}, u32[]{:S(2)}) %collective-permute-start.6) | collective-permute-done | bytes 196640 | tf_op jit(solution)/shard_map/ppermute | solution.py:22
  42.3 1.0 add.211
  43.2 1.5 %collective-permute-start.7 = (f32[3,64,256]{2,1,0:T(8,128)S(1)}, f32[3,64,256]{2,1,0:T(8,128)S(1)}, u32[]{:S(2)}, u32[]{:S(2)}) collective-permute-start(f32[3,64,256]{2,1,0:T(8,128)S(1)} %add.210), channel_id=1, source_target_pairs={{0,8},{8,0},{16,24},{24,16},{1,9},{9,1},{17,25},{25,17},{2,10},{10... | collective-permute-start | bytes 589832 | tf_op jit(solution)/shard_map/ppermute | solution.py:22
  45.2 1.1 select_maximum_fusion.2.refs_6_
  46.3 0.9 fusion.58
  48.1 0.9 collective-permute-done.7
  49.0 1.4 %collective-permute-done.8 = f32[3,64,256]{2,1,0:T(8,128)S(1)} collective-permute-done((f32[3,64,256]{2,1,0:T(8,128)S(1)}, f32[3,64,256]{2,1,0:T(8,128)S(1)}, u32[]{:S(2)}, u32[]{:S(2)}) %collective-permute-start.8) | collective-permute-done | bytes 196640 | tf_op jit(solution)/shard_map/ppermute | solution.py:22
  50.4 1.6 %collective-permute-start.10 = (f32[3,64,256]{2,1,0:T(8,128)S(1)}, f32[3,64,256]{2,1,0:T(8,128)S(1)}, u32[]{:S(2)}, u32[]{:S(2)}) collective-permute-start(f32[3,64,256]{2,1,0:T(8,128)S(1)} %add.218), channel_id=1, source_target_pairs={{0,4},{1,5},{2,6},{3,7},{4,0},{5,1},{6,2},{7,3},{8,12},{9,13},{10,... | collective-permute-start | bytes 589832 | tf_op jit(solution)/shard_map/ppermute | solution.py:22
  52.0 7.1 %collective-permute-done.9 = f32[3,64,256]{2,1,0:T(8,128)S(1)} collective-permute-done((f32[3,64,256]{2,1,0:T(8,128)S(1)}, f32[3,64,256]{2,1,0:T(8,128)S(1)}, u32[]{:S(2)}, u32[]{:S(2)}) %collective-permute-start.9) | collective-permute-done | bytes 196640 | tf_op jit(solution)/shard_map/ppermute | solution.py:22
  59.8 0.8 collective-permute-done.11.refs_2_
  61.3 2.3 %collective-permute-start.14 = (f32[38,2,8,256]{3,2,1,0:T(8,128)S(1)}, f32[38,2,8,256]{3,2,1,0:T(8,128)S(1)}, u32[]{:S(2)}, u32[]{:S(2)}) collective-permute-start(f32[38,2,8,256]{3,2,1,0:T(8,128)S(1)} %get-tuple-element.60), channel_id=1, source_target_pairs={{1,0},{2,1},{3,2},{4,3},{5,4},{6,5},{7,6},{0,7},{9,8},{10,9},{11,1... | collective-permute-start | bytes 1867784 | tf_op jit(solution)/shard_map/ppermute | solution.py:377
  63.6 26.1 %shard_map.101.refs_7_ = bf16[3,5,256,256]{3,2,1,0:T(8,128)(2,1)S(1)} custom-call(f32[3,64,256]{2,1,0:T(8,128)S(1)} %add.219.refs_0_, f32[3,64,256]{2,1,0:T(8,128)S(1)} %add.220.refs_1_, f32[3,64,256]{2,1,0:T(8,128)S(1)} %collective-permute-done.11.refs_2_, f32[3,64,256]{2,1,0:T(8,128)S(1)} %collective-permute-done.12.refs_3_, ...), custom_call_target="tpu_custom_call" | custom-call | flops 3019898880 | bytes 6291456 | tf_op jit(solution)/shard_map/pallas_call | solution.py:229
  89.7 1.3 copy-done.1
  91.0 0.9 copy-done.7
  91.8 0.9 copy-done.8
  92.7 37.4 %shard_map.102 = f32[32,16,8,256]{3,2,1,0:T(8,128)} custom-call(f32[32,16,8,256]{3,2,1,0:T(8,128)} %refs_0_.1, f32[3,16,8,256]{3,2,1,0:T(8,128)} %copy-done.6, f32[3,16,8,256]{3,2,1,0:T(8,128)} %collective-permute-done.2.refs_2_, f32[38,2,8,256]{3,2,1,0:T(8,128)} %copy-done.7, f32[38,2,8,256]{3,2,1,0:T(8,128)} %copy-done.8, ...), custom_call_target="tpu_custom_call" | custom-call | tf_op jit(solution)/shard_map/pallas_call | solution.py:349
  (87 shorter events, 10.0 us)
Async XLA Ops:
  0.8 2.2 %copy-start = (f32[32,16,8,256]{3,2,1,0:T(8,128)S(1)}, f32[32,16,8,256]{3,2,1,0:T(8,128)}, u32[]{:S(2)}) copy-start(f32[32,16,8,256]{3,2,1,0:T(8,128)} %refs_0_.1) | copy-start | bytes 12582916
  4.5 2.1 %copy-start.15 = (s32[3,2]{0,1:T(2,128)S(1)}, s32[3,2]{0,1:T(2,128)}, u32[]{:S(2)}) copy-start(s32[3,2]{0,1:T(2,128)} %param.15) | copy-start | bytes 76
  4.5 2.1 %copy-start.14 = (s32[3]{0:T(128)S(1)}, s32[3]{0:T(128)}, u32[]{:S(2)}) copy-start(s32[3]{0:T(128)} %param.16) | copy-start | bytes 40
  4.5 4.7 %copy-start.3 = (s32[3,256]{1,0:T(4,128)S(1)}, s32[3,256]{1,0:T(4,128)}, u32[]{:S(2)}) copy-start(s32[3,256]{1,0:T(4,128)} %cells.1) | copy-start | bytes 9220
  4.5 4.7 %slice-start = ((s32[3,256]{1,0:T(4,128)}), s32[3,128]{1,0:T(4,128)S(1)}, s32[]{:S(2)}) async-start(s32[3,256]{1,0:T(4,128)} %cells.1), calls=%async_computation | async-start | bytes 4096 | tf_op jit(solution)/shard_map/slice | solution.py:434
  4.5 4.9 %copy-start.13 = (f32[3,256]{1,0:T(4,128)S(1)}, f32[3,256]{1,0:T(4,128)}, u32[]{:S(2)}) copy-start(f32[3,256]{1,0:T(4,128)} %param.13) | copy-start | bytes 9220
  4.5 4.9 %slice-start.3 = ((f32[3,256]{1,0:T(4,128)}), f32[3,128]{1,0:T(4,128)S(1)}, s32[]{:S(2)}) async-start(f32[3,256]{1,0:T(4,128)} %param.13), calls=%async_computation.3 | async-start | bytes 4096 | tf_op jit(solution)/shard_map/slice | solution.py:434
  4.5 4.9 %copy-start.9 = (f32[32,16,8]{0,2,1:T(8,128)S(1)}, f32[32,16,8]{0,2,1:T(8,128)}, u32[]{:S(2)}) copy-start(f32[32,16,8]{0,2,1:T(8,128)} %param.19) | copy-start | bytes 49156
  4.5 4.9 %copy-start.10 = (f32[32,16,8]{0,2,1:T(8,128)S(1)}, f32[32,16,8]{0,2,1:T(8,128)}, u32[]{:S(2)}) copy-start(f32[32,16,8]{0,2,1:T(8,128)} %param.18) | copy-start | bytes 49156
  4.6 4.9 %copy-start.11 = (f32[32,16,8]{0,2,1:T(8,128)S(1)}, f32[32,16,8]{0,2,1:T(8,128)}, u32[]{:S(2)}) copy-start(f32[32,16,8]{0,2,1:T(8,128)} %param.17) | copy-start | bytes 49156
  4.6 1.9 %collective-permute-start = (f32[3,128,256]{2,1,0:T(8,128)S(1)}, f32[3,128,256]{2,1,0:T(8,128)S(1)}, u32[]{:S(2)}, u32[]{:S(2)}) collective-permute-start(f32[3,128,256]{2,1,0:T(8,128)S(1)} %get-tuple-element.38), channel_id=1, source_target_pairs={{0,1},{1,0},{2,3},{3,2},{4,5},{5,4},{6,7},{7,6},{8,9},{9,8},{10,11... | collective-permute-start | bytes 1179656 | tf_op jit(solution)/shard_map/ppermute | solution.py:22
  11.4 12.1 %collective-permute-start.4 = (f32[3,64,256]{2,1,0:T(8,128)S(1)}, f32[3,64,256]{2,1,0:T(8,128)S(1)}, u32[]{:S(2)}, u32[]{:S(2)}) collective-permute-start(f32[3,64,256]{2,1,0:T(8,128)S(1)} %get-tuple-element.83), channel_id=1, source_target_pairs={{0,8},{8,0},{16,24},{24,16},{1,9},{9,1},{17,25},{25,17},{2,10},{10... | collective-permute-start | bytes 589832 | tf_op jit(solution)/shard_map/ppermute | solution.py:22
  14.3 9.2 %collective-permute-start.3 = (f32[3,64,256]{2,1,0:T(8,128)S(1)}, f32[3,64,256]{2,1,0:T(8,128)S(1)}, u32[]{:S(2)}, u32[]{:S(2)}) collective-permute-start(f32[3,64,256]{2,1,0:T(8,128)S(1)} %get-tuple-element.84), channel_id=1, source_target_pairs={{0,2},{1,3},{2,0},{3,1},{4,6},{5,7},{6,4},{7,5},{8,10},{9,11},{10,... | collective-permute-start | bytes 589832 | tf_op jit(solution)/shard_map/ppermute | solution.py:22
  15.9 14.3 %collective-permute-start.1 = (f32[3,16,8,256]{3,2,1,0:T(8,128)S(1)}, f32[3,16,8,256]{3,2,1,0:T(8,128)S(1)}, u32[]{:S(2)}, u32[]{:S(2)}) collective-permute-start(f32[3,16,8,256]{3,2,1,0:T(8,128)S(1)} %select_maximum_fusion.1), channel_id=1, source_target_pairs={{0,8},{8,16},{16,24},{1,9},{9,17},{17,25},{2,10},{10,18},{18,26},{... | collective-permute-start | bytes 1179656 | tf_op jit(solution)/shard_map/ppermute | solution.py:377
  19.0 2.7 %copy-start.12 = (f32[3,256]{1,0:T(4,128)S(1)}, f32[3,256]{1,0:T(4,128)}, u32[]{:S(2)}) copy-start(f32[3,256]{1,0:T(4,128)} %param.11) | copy-start | bytes 9220
  19.0 2.7 %slice-start.2 = ((f32[3,256]{1,0:T(4,128)}), f32[3,128]{1,0:T(4,128)S(1)}, s32[]{:S(2)}) async-start(f32[3,256]{1,0:T(4,128)} %param.11), calls=%async_computation.2 | async-start | bytes 4096 | tf_op jit(solution)/shard_map/slice | solution.py:434
  19.0 13.7 %collective-permute-start.2 = (f32[3,16,8,256]{3,2,1,0:T(8,128)}, f32[3,16,8,256]{3,2,1,0:T(8,128)}, u32[]{:S(2)}, u32[]{:S(2)}) collective-permute-start(f32[3,16,8,256]{3,2,1,0:T(8,128)} %select_maximum_fusion), channel_id=1, source_target_pairs={{8,0},{16,8},{24,16},{9,1},{17,9},{25,17},{10,2},{18,10},{26,18},{... | collective-permute-start | bytes 1179656 | tf_op jit(solution)/shard_map/ppermute | solution.py:377
  21.7 8.2 %copy-start.4 = (f32[3,256,256]{2,1,0:T(8,128)S(1)}, f32[3,256,256]{2,1,0:T(8,128)}, u32[]{:S(2)}) copy-start(f32[3,256,256]{2,1,0:T(8,128)} %param.12) | copy-start | bytes 2359300
  21.7 8.2 %slice-start.1 = ((f32[3,256,256]{2,1,0:T(8,128)}), f32[3,128,256]{2,1,0:T(8,128)S(1)}, s32[]{:S(2)}) async-start(f32[3,256,256]{2,1,0:T(8,128)} %param.12), calls=%async_computation.1 | async-start | bytes 786432 | tf_op jit(solution)/shard_map/slice | solution.py:434
  23.6 11.6 %collective-permute-start.5 = (f32[3,64,256]{2,1,0:T(8,128)S(1)}, f32[3,64,256]{2,1,0:T(8,128)}, u32[]{:S(2)}, u32[]{:S(2)}) collective-permute-start(f32[3,64,256]{2,1,0:T(8,128)S(1)} %get-tuple-element.48), channel_id=1, source_target_pairs={{0,4},{1,5},{2,6},{3,7},{4,0},{5,1},{6,2},{7,3},{8,12},{9,13},{10,... | collective-permute-start | bytes 589832 | tf_op jit(solution)/shard_map/ppermute | solution.py:22
  27.4 14.8 %collective-permute-start.6 = (f32[3,64,256]{2,1,0:T(8,128)S(1)}, f32[3,64,256]{2,1,0:T(8,128)}, u32[]{:S(2)}, u32[]{:S(2)}) collective-permute-start(f32[3,64,256]{2,1,0:T(8,128)S(1)} %get-tuple-element.49), channel_id=1, source_target_pairs={{0,16},{8,24},{16,0},{24,8},{1,17},{9,25},{17,1},{25,9},{2,18},{10... | collective-permute-start | bytes 589832 | tf_op jit(solution)/shard_map/ppermute | solution.py:22
  43.2 5.7 %collective-permute-start.7 = (f32[3,64,256]{2,1,0:T(8,128)S(1)}, f32[3,64,256]{2,1,0:T(8,128)S(1)}, u32[]{:S(2)}, u32[]{:S(2)}) collective-permute-start(f32[3,64,256]{2,1,0:T(8,128)S(1)} %add.210), channel_id=1, source_target_pairs={{0,8},{8,0},{16,24},{24,16},{1,9},{9,1},{17,25},{25,17},{2,10},{10... | collective-permute-start | bytes 589832 | tf_op jit(solution)/shard_map/ppermute | solution.py:22
  44.7 5.7 %collective-permute-start.8 = (f32[3,64,256]{2,1,0:T(8,128)S(1)}, f32[3,64,256]{2,1,0:T(8,128)S(1)}, u32[]{:S(2)}, u32[]{:S(2)}) collective-permute-start(f32[3,64,256]{2,1,0:T(8,128)S(1)} %add.211), channel_id=1, source_target_pairs={{0,2},{1,3},{2,0},{3,1},{4,6},{5,7},{6,4},{7,5},{8,10},{9,11},{10,... | collective-permute-start | bytes 589832 | tf_op jit(solution)/shard_map/ppermute | solution.py:22
  46.3 43.3 %copy-start.5 = (f32[3,16,8,128]{3,2,1,0:T(8,128)}, f32[3,16,8,128]{3,2,1,0:T(8,128)S(1)}, u32[]{:S(2)}) copy-start(f32[3,16,8,128]{3,2,1,0:T(8,128)S(1)} %select_maximum_fusion.2.refs_6_) | copy-start | bytes 589828
  50.4 8.7 %collective-permute-start.9 = (f32[3,64,256]{2,1,0:T(8,128)S(1)}, f32[3,64,256]{2,1,0:T(8,128)S(1)}, u32[]{:S(2)}, u32[]{:S(2)}) collective-permute-start(f32[3,64,256]{2,1,0:T(8,128)S(1)} %add.217), channel_id=1, source_target_pairs={{0,16},{8,24},{16,0},{24,8},{1,17},{9,25},{17,1},{25,9},{2,18},{10... | collective-permute-start | bytes 589832 | tf_op jit(solution)/shard_map/ppermute | solution.py:22
  50.4 8.8 %collective-permute-start.10 = (f32[3,64,256]{2,1,0:T(8,128)S(1)}, f32[3,64,256]{2,1,0:T(8,128)S(1)}, u32[]{:S(2)}, u32[]{:S(2)}) collective-permute-start(f32[3,64,256]{2,1,0:T(8,128)S(1)} %add.218), channel_id=1, source_target_pairs={{0,4},{1,5},{2,6},{3,7},{4,0},{5,1},{6,2},{7,3},{8,12},{9,13},{10,... | collective-permute-start | bytes 589832 | tf_op jit(solution)/shard_map/ppermute | solution.py:22
  59.1 1.5 %collective-permute-start.11 = (f32[3,64,256]{2,1,0:T(8,128)S(1)}, f32[3,64,256]{2,1,0:T(8,128)S(1)}, u32[]{:S(2)}, u32[]{:S(2)}) collective-permute-start(f32[3,64,256]{2,1,0:T(8,128)S(1)} %add.219.refs_0_), channel_id=1, source_target_pairs={{0,1},{1,0},{2,3},{3,2},{4,5},{5,4},{6,7},{7,6},{8,9},{9,8},{10,11... | collective-permute-start | bytes 589832 | tf_op jit(solution)/shard_map/ppermute | solution.py:22
  59.3 1.7 %collective-permute-start.12 = (f32[3,64,256]{2,1,0:T(8,128)S(1)}, f32[3,64,256]{2,1,0:T(8,128)S(1)}, u32[]{:S(2)}, u32[]{:S(2)}) collective-permute-start(f32[3,64,256]{2,1,0:T(8,128)S(1)} %add.220.refs_1_), channel_id=1, source_target_pairs={{0,1},{1,0},{2,3},{3,2},{4,5},{5,4},{6,7},{7,6},{8,9},{9,8},{10,11... | collective-permute-start | bytes 589832 | tf_op jit(solution)/shard_map/ppermute | solution.py:22
  60.9 30.0 %collective-permute-start.13 = (f32[38,2,8,256]{3,2,1,0:T(8,128)S(1)}, f32[38,2,8,256]{3,2,1,0:T(8,128)S(1)}, u32[]{:S(2)}, u32[]{:S(2)}) collective-permute-start(f32[38,2,8,256]{3,2,1,0:T(8,128)S(1)} %get-tuple-element.59), channel_id=1, source_target_pairs={{0,1},{1,2},{2,3},{3,4},{4,5},{5,6},{6,7},{7,0},{8,9},{9,10},{10,1... | collective-permute-start | bytes 1867784 | tf_op jit(solution)/shard_map/ppermute | solution.py:377
  61.3 29.7 %collective-permute-start.14 = (f32[38,2,8,256]{3,2,1,0:T(8,128)S(1)}, f32[38,2,8,256]{3,2,1,0:T(8,128)S(1)}, u32[]{:S(2)}, u32[]{:S(2)}) collective-permute-start(f32[38,2,8,256]{3,2,1,0:T(8,128)S(1)} %get-tuple-element.60), channel_id=1, source_target_pairs={{1,0},{2,1},{3,2},{4,3},{5,4},{6,5},{7,6},{0,7},{9,8},{10,9},{11,1... | collective-permute-start | bytes 1867784 | tf_op jit(solution)/shard_map/ppermute | solution.py:377
  89.7 1.3 %copy-start.1 = (bf16[3,5,256,256]{3,2,1,0:T(8,128)(2,1)}, bf16[3,5,256,256]{3,2,1,0:T(8,128)(2,1)S(1)}, u32[]{:S(2)}) copy-start(bf16[3,5,256,256]{3,2,1,0:T(8,128)(2,1)S(1)} %shard_map.101.refs_7_) | copy-start | bytes 5898244
  91.0 0.9 copy-start.7
  (3 other events, 2.3 us)

commit v3 on v2

--- a/solution.py
+++ b/solution.py
@@ -15,6 +15,11 @@
 F32 = jnp.float32
 BF16 = jnp.bfloat16
 VMEM = pl.BlockSpec(memory_space=pltpu.VMEM)
+HBM = pl.BlockSpec(memory_space=pltpu.HBM)
+
+
+def in_hbm(x):
+    return pltpu.with_memory_space_constraint(x, pltpu.HBM)
 
 
 def shifted(x, axis, flip):
@@ -30,68 +35,69 @@
     return out
 
 
-def gather_kernel(cells, tiles, spot, state_hbm, first_ref, second_ref, state_ref, sem):
-    count, half, members = first_ref.shape
-    core = lax.rem(spot[1], 2)
-
-    def owned(b):
-        return jnp.logical_and(tiles[b, 0] == spot[0], tiles[b, 1] == spot[1])
-
-    any_owned = owned(0)
-    for b in range(1, count):
-        any_owned = jnp.logical_or(any_owned, owned(b))
-
-    @pl.when(any_owned)
-    def _():
-        copy = pltpu.make_async_copy(state_hbm, state_ref, sem)
+def gather_kernel(cells_hbm, tiles_hbm, state_hbm, *refs):
+    first_ref, second_ref, cells, tiles, state_ref, sems = refs
+    pairs = ((tiles_hbm, tiles), (cells_hbm, cells), (state_hbm, state_ref))
+    copies = [pltpu.make_async_copy(x, to, sems.at[n]) for n, (x, to) in enumerate(pairs)]
+    for copy in copies:
         copy.start()
+    parts, count, rows, members = first_ref.shape
+    lat, lon = lax.axis_index("lat"), lax.axis_index("lon")
+    core = lax.rem(lon, 2)
+    first_ref[...] = jnp.zeros(first_ref.shape, F32)
+    second_ref[...] = jnp.zeros(second_ref.shape, F32)
+    for copy in copies:
         copy.wait()
-
     for b in range(count):
-        mine = owned(b)
-        for side, ref in enumerate((first_ref, second_ref)):
-            start = lax.rem(core + side, 2) * half
-
-            @pl.when(mine)
-            def _():
-                @pl.loop(0, half // 8)
-                def _(i):
-                    for n in range(8):
-                        row = state_ref[pl.ds(cells[b, start + i * 8 + n], 1), :]
-                        ref[b, pl.ds(i * 8 + n, 1), :] = row
-
-            @pl.when(jnp.logical_not(mine))
-            def _():
-                ref[b] = jnp.zeros((half, members), F32)
-
-
-def gather(ensemble, cells, tiles, spot):
+
+        @pl.when(jnp.logical_and(tiles[0, b] == lat, tiles[1, b] == lon))
+        def _():
+            for side, ref in enumerate((first_ref, second_ref)):
+                for part in range(parts):
+                    start = (lax.rem(core + side, 2) * parts + part) * rows
+
+                    @pl.loop(0, rows // 8)
+                    def _(i):
+                        for n in range(8):
+                            cell = cells[b, start + i * 8 + n]
+                            ref[part, b, pl.ds(i * 8 + n, 1), :] = state_ref[pl.ds(cell, 1), :]
+
+
+def gather(ensemble, cells, tiles):
     members = ensemble.shape[-1]
     flat = ensemble.reshape(-1, members)
     count, nobs = cells.shape
-    smem = pl.BlockSpec(memory_space=pltpu.SMEM)
-    out = jax.ShapeDtypeStruct((count, nobs // 2, members), F32)
+    out = jax.ShapeDtypeStruct((2, count, nobs // 4, members), F32)
     return pl.pallas_call(
         gather_kernel,
         out_shape=[out, out],
-        in_specs=[smem] * 3 + [pl.BlockSpec(memory_space=pl.ANY)],
+        in_specs=[HBM] * 3,
         out_specs=[VMEM] * 2,
-        scratch_shapes=[pltpu.VMEM(flat.shape, F32), pltpu.SemaphoreType.DMA],
+        scratch_shapes=[
+            pltpu.SMEM(cells.shape, jnp.int32),
+            pltpu.SMEM(tiles.shape[::-1], jnp.int32),
+            pltpu.VMEM(flat.shape, F32),
+            pltpu.SemaphoreType.DMA((3,)),
+        ],
         compiler_params=pltpu.CompilerParams(vmem_limit_bytes=24 << 20),
-    )(cells, tiles, spot, flat)
-
-
-def spread_out(mine, half, fillers):
-    fillers, made = list(fillers), []
-    a, b = mine[:, :half], mine[:, half:]
+    )(*map(in_hbm, (cells, tiles.T, flat)))
+
+
+def spread_out(a, b, fillers):
     lon, lat = stages("lon", 2), stages("lat", 1)
-    for (a_axis, a_flip), (b_axis, b_flip) in zip(lon + lat, lat + lon):
+    hops, made = list(zip(lon + lat, lat + lon)), []
+    for n, ((a_axis, a_flip), (b_axis, b_flip)) in enumerate(hops):
         a_moved, b_moved = shifted(a, a_axis, a_flip), shifted(b, b_axis, b_flip)
+        filler = fillers[n] if n < len(fillers) else None
+        if filler is not None:
+            function, args = filler
+            args = args(made) if callable(args) else args
+            a, b, args = lax.optimization_barrier((a, b, args))
+            made.append(function(*args))
         a, b = a + a_moved, b + b_moved
-        if fillers:
-            a, b, filler = lax.optimization_barrier((a, b, fillers.pop(0)))
-            made.append(filler)
-    return (a, b, shifted(a, "lon", 1), shifted(b, "lon", 1)), made + fillers
+        if filler is not None and n:
+            a, b, made[n] = lax.optimization_barrier((a, b, made[n]))
+    return (a, b, shifted(a, "lon", 1), shifted(b, "lon", 1)), made
 
 
 def taper(lat_a, lon_a, lat_b, lon_b, radius, total_lon):
@@ -230,7 +236,7 @@
         solve_kernel,
         out_shape=jax.ShapeDtypeStruct(out, BF16),
         in_specs=[VMEM] * 7,
-        out_specs=pl.BlockSpec(memory_space=pl.ANY),
+        out_specs=HBM,
         scratch_shapes=[
             pltpu.VMEM((count, nobs, members), F32),
             pltpu.VMEM(out, BF16),
@@ -270,33 +276,29 @@
     coef_ref, wide_ref, z_ref, out_ref, sems, out_sem = refs[7:]
     count = factor_ref.shape[0]
     tall, wide, levels, members = x_ref.shape
-    inner = (pl.ds(HALO, tall - 2 * HALO), pl.ds(HALO, wide - 2 * HALO))
-    places = (
-        inner,
-        (pl.ds(0, HALO), inner[1]),
-        (pl.ds(tall - HALO, HALO), inner[1]),
-        (slice(None), pl.ds(0, HALO)),
-        (slice(None), pl.ds(wide - HALO, HALO)),
-    )
-    heights = (tall - 2 * HALO, HALO, HALO, tall, tall)
-    copies = [
-        pltpu.make_async_copy(piece.at[pl.ds(0, height)], x_ref.at[place], sems.at[n])
-        for n, (piece, place, height) in enumerate(zip(pieces, places, heights))
-    ]
-    copies.append(pltpu.make_async_copy(taper_hbm, taper_ref, sems.at[5]))
-    copies.append(pltpu.make_async_copy(factor_hbm, factor_ref, sems.at[13]))
-    coef_copies = [
-        pltpu.make_async_copy(coef_hbm, coef_ref.at[:, pl.ds(1, wide - 4)], sems.at[6])
-    ]
+    span = wide - 2 * HALO
+    inner = pl.ds(HALO, span)
+    moves = [(pieces[0], x_ref.at[pl.ds(HALO, tall - 2 * HALO), inner])]
+    for n in range(HALO):
+        rows = pl.ds(n * span, span)
+        moves.append((pieces[1].at[rows], x_ref.at[n, inner]))
+        moves.append((pieces[2].at[rows], x_ref.at[tall - HALO + n, inner]))
+    for n in range(2):
+        to = x_ref.at[:, pl.ds(n * (wide - HALO), HALO)]
+        moves.append((pieces[3 + n].at[pl.ds(0, tall)], to))
+    moves += [(taper_hbm, taper_ref), (factor_hbm, factor_ref)]
+    moves.append((coef_hbm, coef_ref.at[:, pl.ds(1, wide - 4)]))
     for n in range(3):
         for side in range(2):
             source = pieces[3 + side].at[tall + n // 2, n % 2, :, pl.ds(0, coef_ref.shape[-1])]
-            to = coef_ref.at[n, side * (wide - 3)]
-            coef_copies.append(pltpu.make_async_copy(source, to, sems.at[7 + 2 * n + side]))
-    for copy in copies + coef_copies:
+            moves.append((source, coef_ref.at[n, side * (wide - 3)]))
+    copies = [pltpu.make_async_copy(x, to, sems.at[n]) for n, (x, to) in enumerate(moves)]
+    for copy in copies:
         copy.start()
     for copy in copies:
         copy.wait()
+
+    columns = -(-(wide - 2) * chunk // tall)
 
     @pl.loop(0, tall // chunk)
     def _(i):
@@ -309,19 +311,17 @@
             gain = gain.reshape(chunk * wide * levels, -1)
             x = x + split_dot(gain, factor_ref[b, 2], factor_ref[b, 3], factor_ref[b, 4])
         x_ref[at] = x.reshape(chunk, wide, levels, members)
-
-    for copy in coef_copies:
-        copy.wait()
+        for n in range(columns):
+            j = jnp.minimum(i * columns + n, wide - 3)
+            tiles = [coef_ref[kind, j] for kind in range(3)]
+            for row in range(tall - 2):
+                for kind, coef in enumerate(five(*[lane_spread(t, row) for t in tiles])):
+                    wide_ref[kind, row, j] = coef
 
     @pl.loop(0, wide - 2)
     def _(j):
-        tiles = five(*[coef_ref[n, j] for n in range(3)])
-
         def coef_at(i):
-            found = [jnp.broadcast_to(tile[:, i : i + 1], (levels, LANES)) for tile in tiles]
-            for n, coef in enumerate(found):
-                wide_ref[n, i, j] = coef
-            return found
+            return [wide_ref[n, i, j] for n in range(5)]
 
         def store(i, value):
             z_ref[i, j] = value
@@ -345,12 +345,11 @@
 def move(pieces, tapers, coefs, factors):
     tall, wide = pieces[0].shape[0] + 2 * HALO, pieces[0].shape[1] + 2 * HALO
     levels, members = pieces[0].shape[2:]
-    hbm = pl.BlockSpec(memory_space=pl.ANY)
     return pl.pallas_call(
         functools.partial(move_kernel, 12 if tall % 12 == 0 else 1),
         out_shape=jax.ShapeDtypeStruct(pieces[0].shape, F32),
-        in_specs=[hbm] * 8,
-        out_specs=hbm,
+        in_specs=[HBM] * 8,
+        out_specs=HBM,
         scratch_shapes=[
             pltpu.VMEM((tall, wide, levels, members), F32),
             pltpu.VMEM(tapers.shape, F32),
@@ -359,11 +358,11 @@
             pltpu.VMEM((5, tall - 2, wide - 2, levels, LANES), F32),
             pltpu.VMEM((tall - 2, wide - 2, levels, members), F32),
             pltpu.VMEM(pieces[0].shape, F32),
-            pltpu.SemaphoreType.DMA((14,)),
+            pltpu.SemaphoreType.DMA((10 + 2 * HALO + 6,)),
             pltpu.SemaphoreType.DMA,
         ],
         compiler_params=pltpu.CompilerParams(vmem_limit_bytes=60 << 20),
-    )(*pieces, tapers, coefs, factors)
+    )(*map(in_hbm, (*pieces, tapers, coefs, factors)))
 
 
 def lanes(x, count):
@@ -397,96 +396,85 @@
 
     core = lon_index % 2
     half = nobs // 2
-    spot = jnp.stack([lat_index, lon_index])
-    mine, others = gather(ensemble, obs_cells, owner_tiles, spot)
-    mine = mine + shifted(others, "lon", 1)
-    (
-        mine,
-        obs_cells,
-        obs_values,
-        obs_var,
-        obs_noise,
-        owner_tiles,
-        radius,
-        courant_lat,
-        courant_lon,
-        diffusivity,
-        south,
-        north,
-    ) = lax.optimization_barrier(
-        (
-            mine,
-            obs_cells,
-            obs_values,
-            obs_var,
-            obs_noise,
-            owner_tiles,
-            radius,
-            courant_lat,
-            courant_lon,
-            diffusivity,
-            ensemble[-HALO:],
-            ensemble[:HALO],
-        )
-    )
-
+    mine, others = gather(ensemble, obs_cells, owner_tiles)
+    others = shifted(others, "lon", 1)
+    a, b = mine[0] + others[0], mine[1] + others[1]
     def own_first(x):
         x = jnp.concatenate([x, x[:, :half]], axis=1)
         return lax.dynamic_slice_in_dim(x, core * half, nobs, 1)
 
-    obs_cells, obs_values, obs_var, obs_noise = map(
-        own_first, (obs_cells, obs_values, obs_var, obs_noise)
-    )
-
-    speeds = jnp.stack([courant_lat, courant_lon, diffusivity]).transpose(0, 2, 3, 1)
-    thin = lanes(speeds[..., -1:].transpose(3, 1, 2, 0), members)
-    south = jnp.concatenate([south, thin])
-    thin = lanes(speeds[..., :1].transpose(3, 1, 2, 0), members)
-    north = jnp.concatenate([north, thin])
-    south, north = neighbours(south, north, "lat", False)
-    south_thin, north_thin = (
-        side[HALO:, :, :, :3].transpose(3, 1, 2, 0) for side in (south, north)
-    )
-    speeds = jnp.concatenate([south_thin, speeds, north_thin], axis=-1)
-    speeds = lanes(speeds, LANES)
+    def lat_edges(ensemble, *speeds):
+        speeds = jnp.stack(speeds).transpose(0, 2, 3, 1)
+
+        def with_thin(edge, thin):
+            thin = lanes(thin.transpose(2, 0, 1).reshape(levels, -1), members)
+            return jnp.concatenate([edge.reshape((-1,) + edge.shape[2:]), thin[None]])
+
+        south = with_thin(ensemble[-HALO:], speeds[..., -1])
+        north = with_thin(ensemble[:HALO], speeds[..., 0])
+        return speeds, *neighbours(south, north, "lat", False)
 
     tall, wide = ensemble.shape[0] + 2 * HALO, ensemble.shape[1] + 2 * HALO
-    place = obs_cells // levels
-    obs_lat = owner_tiles[:, :1] * CLAT + place // CLON
-    obs_lon = owner_tiles[:, 1:] * CLON + place % CLON
-    lat_cells = lat_index * CLAT - HALO + jnp.arange(tall, dtype=jnp.int32)
-    lon_cells = lon_index * CLON - HALO + jnp.arange(wide, dtype=jnp.int32)
-    lon_cells = (lon_cells + total_lon) % total_lon
-    lat_cells = jnp.broadcast_to(lat_cells[:, None], (tall, wide)).reshape(-1)
-    lon_cells = jnp.broadcast_to(lon_cells[None, :], (tall, wide)).reshape(-1)
-    tapers = jnp.stack(
-        [
+
+    def obs_places(cells, tiles):
+        place = own_first(cells) // levels
+        return tiles[:, :1] * CLAT + place // CLON, tiles[:, 1:] * CLON + place % CLON
+
+    def cell_tapers(cells, tiles, radius):
+        obs_lat, obs_lon = obs_places(cells, tiles)
+        lat_cells = lat_index * CLAT - HALO + jnp.arange(tall, dtype=jnp.int32)
+        lon_cells = lon_index * CLON - HALO + jnp.arange(wide, dtype=jnp.int32)
+        lon_cells = (lon_cells + total_lon) % total_lon
+        lat_cells = jnp.broadcast_to(lat_cells[:, None], (tall, wide)).reshape(-1)
+        lon_cells = jnp.broadcast_to(lon_cells[None, :], (tall, wide)).reshape(-1)
+        tapers = [
             taper(lat_cells, lon_cells, obs_lat[b], obs_lon[b], radius[b], total_lon)
             for b in range(NBATCH)
         ]
-    ).reshape(NBATCH, tall, wide, nobs) / (members - 1)
-    mutual = jnp.stack(
-        [
+        return jnp.stack(tapers).reshape(NBATCH, tall, wide, nobs) / (members - 1)
+
+    def lon_edges(ensemble, speeds, south, north):
+        def thin_of(side):
+            thin = side[-1, :, : 3 * ensemble.shape[1]].reshape(levels, 3, -1)
+            return thin.transpose(1, 2, 0)[..., None]
+
+        speeds = jnp.concatenate([thin_of(south), speeds, thin_of(north)], axis=-1)
+        speeds = lanes(speeds, LANES)
+        shape = (HALO,) + ensemble.shape[1:]
+        rows = (south[:-1].reshape(shape), ensemble, north[:-1].reshape(shape))
+
+        def side(at, extent, lane):
+            edge = jnp.concatenate([part[:, at:extent] for part in rows])
+            tile = lanes(speeds[:, lane], members)
+            tile = jnp.pad(tile, ((0, 1), (0, 0), (0, 0))).reshape((2, 2) + tile.shape[1:])
+            return jnp.concatenate([edge, tile])
+
+        last = ensemble.shape[1]
+        return speeds, side(last - HALO, last, last - 1), side(0, HALO, 0)
+
+    def obs_terms(cells, tiles, radius, values, noise, variance):
+        obs_lat, obs_lon = obs_places(cells, tiles)
+        mutual = [
             taper(obs_lat[c], obs_lon[c], obs_lat[b], obs_lon[b], radius[b], total_lon)
             for b, c in ((0, 1), (0, 2), (1, 2))
         ]
-    ) / (members - 1)
-    target = obs_values[:, :, None] + jnp.sqrt(obs_var)[:, :, None] * obs_noise
-
-    def side(at, extent, lane):
-        edge = jnp.concatenate([part[:, at:extent] for part in (south[:HALO], ensemble, north[:HALO])])
-        tile = lanes(speeds[:, lane], members)
-        tile = jnp.pad(tile, ((0, 1), (0, 0), (0, 0))).reshape((2, 2) + tile.shape[1:])
-        return jnp.concatenate([edge, tile])
-
-    last = ensemble.shape[1]
-    before, after = side(last - HALO, last, last - 1), side(0, HALO, 0)
-    pieces, (tapers, (target, mutual), (speeds, before, after)) = spread_out(
-        mine, half // 2, (tapers, (target, mutual), (speeds, before, after))
+        values, noise, variance = map(own_first, (values, noise, variance))
+        target = values[:, :, None] + jnp.sqrt(variance)[:, :, None] * noise
+        return target, variance, jnp.stack(mutual) / (members - 1)
+
+    pieces, made = spread_out(
+        a,
+        b,
+        (
+            (lat_edges, (ensemble, courant_lat, courant_lon, diffusivity)),
+            (cell_tapers, (obs_cells, owner_tiles, radius)),
+            (lon_edges, lambda made: (ensemble, *made[0])),
+            (obs_terms, (obs_cells, owner_tiles, radius, obs_values, obs_noise, obs_var)),
+        ),
     )
-    pieces, before, after = lax.optimization_barrier((pieces, before, after))
+    (_, south, north), tapers, (speeds, before, after), (target, variance, mutual) = made
     west, east = neighbours(before, after, "lon", True)
-    factors = solve(pieces, target, obs_var, mutual)
+    factors = solve(pieces, target, variance, mutual)
     cells = (ensemble, south, north, west, east)
     return move(cells, tapers, speeds, factors)
 

time: 131 us -> 114 us (0.87)
  local copies, waits for them, and re-layouts: 16.4 us -> 8.12 us
  other arithmetic: 7.64 us -> 4.13 us
  waiting for transfers between devices: 17.4 us -> 14.4 us
  starting transfers between devices: 22.1 us -> 20.7 us
    unnamed x37 -> x30, local copies, waits for them, and re-layouts: 11.7 us -> 3.03 us
    pallas_call x1, Pallas kernels: 37.4 us -> 34.6 us  [move(): pl.pallas_call(functools.partial(move_kernel, 12 if tall % 12 == 0 else 1...]
    ppermute x11, waiting for transfers between devices: 16.5 us -> 14.4 us  [shifted(): return lax.ppermute(x, axis, [(i, i ^ flip) for i in range(size)])]
    add x7 -> x8, other arithmetic: 2.08 us -> 0.2 us  [spread_out(): a, b = (a + a_moved, b + b_moved)]
    concatenate x4 -> x3, other arithmetic: 1.91 us -> 0.21 us  [the longest x1 0.17 us: lon_edges(): speeds = jnp.concatenate([thin_of(south), speeds, thin_of(north)], axis=-1)]
    pallas_call x1, Pallas kernels: 0.74 us -> 2.26 us  [gather(): pl.pallas_call(gather_kernel, out_shape=[out, out], in_specs=[HBM] * 3, o...]
    slice x10 -> x17, local copies, waits for them, and re-layouts: 4.5 us -> 4.24 us  [the longest x3 1.4 us: lat_edges(): north = with_thin(ensemble[:HALO], speeds[..., 0])]
  transfers between devices with their start and end apart: 15 -> 15, of which waited for: 7 -> 6; matrix products, arithmetic and copies ran while one was open for 10% -> 8% of each run, Pallas kernels for 20% -> 23%
where the time goes in v3:
time: 114 us
  Pallas kernels  63.1 us (55%)
  starting transfers between devices  20.7 us (18%)
  waiting for transfers between devices  14.4 us (13%)
  local copies, waits for them, and re-layouts  8.12 us (7%)
  other arithmetic  4.13 us (4%)
  between operations  3.79 us (3%)
    pallas_call x1, Pallas kernels, move(): pl.pallas_call(functools.partial(move_kernel, 12 if tall % 12 == 0 else 1...  34.6 us
    pallas_call x1, Pallas kernels, solve(): pl.pallas_call(solve_kernel, out_shape=jax.ShapeDtypeStruct(out, BF16), i...  26.2 us
    ppermute x11, waiting for transfers between devices, shifted(): return lax.ppermute(x, axis, [(i, i ^ flip) for i in range(size)])  14.4 us
    ppermute x11, starting transfers between devices, shifted(): return lax.ppermute(x, axis, [(i, i ^ flip) for i in range(size)])  14.4 us
    ppermute x4, starting transfers between devices, neighbours(): return (lax.ppermute(before, axis, up), lax.ppermute(after, axis, down))  6.3 us
    unnamed x30, local copies, waits for them, and re-layouts  3.03 us
  transfers between devices with their start and end apart: 15, of which 6 were waited for; matrix products, arithmetic and copies ran while one was open for 8% of the time, Pallas kernels for 23%

profile of v3, /device:TPU:0, one launch (start us, length us, event | category | flops | bytes accessed | tf_op | source)
XLA Modules:
  0.0 114.2 jit_solution(11844294493637670503)
XLA Ops:
  0.0 2.3 %shard_map.100 = (f32[2,3,64,256]{3,2,1,0:T(8,128)S(1)}, f32[2,3,64,256]{3,2,1,0:T(8,128)S(1)}) custom-call(s32[3,256]{1,0:T(4,128)} %cells_hbm.1, s32[2,3]{1,0:T(2,128)} %bitcast.78, f32[4096,256]{1,0:T(8,128)} %bitcast.62), custom_call_target="tpu_custom_call" | custom-call | tf_op jit(solution)/shard_map/pallas_call | solution.py:71
  2.3 0.6 collective-permute-start
  2.8 1.3 %collective-permute-done = f32[2,3,64,256]{3,2,1,0:T(8,128)S(1)} collective-permute-done((f32[2,3,64,256]{3,2,1,0:T(8,128)S(1)}, f32[2,3,64,256]{3,2,1,0:T(8,128)S(1)}, u32[]{:S(2)}, u32[]{:S(2)}) %collective-permute-start) | collective-permute-done | bytes 393248 | tf_op jit(solution)/shard_map/ppermute | solution.py:27
  4.3 4.2 %collective-permute-start.4 = (f32[3,64,256]{2,1,0:T(8,128)S(1)}, f32[3,64,256]{2,1,0:T(8,128)S(1)}, u32[]{:S(2)}, u32[]{:S(2)}) collective-permute-start(f32[3,64,256]{2,1,0:T(8,128)S(1)} %get-tuple-element.52), channel_id=1, source_target_pairs={{0,8},{8,0},{16,24},{24,16},{1,9},{9,1},{17,25},{25,17},{2,10},{10... | collective-permute-start | bytes 589832 | tf_op jit(solution)/shard_map/ppermute | solution.py:27
  8.5 0.3 collective-permute-start.3
  9.6 1.1 fusion.65
  10.7 2.4 %collective-permute-start.1 = (f32[33,8,256]{2,1,0:T(8,128)S(1)}, f32[33,8,256]{2,1,0:T(8,128)S(1)}, u32[]{:S(2)}, u32[]{:S(2)}) collective-permute-start(f32[33,8,256]{2,1,0:T(8,128)S(1)} %pad_maximum_fusion.2), channel_id=1, source_target_pairs={{0,8},{8,16},{16,24},{1,9},{9,17},{17,25},{2,10},{10,18},{18,26},{... | collective-permute-start | bytes 811016 | tf_op jit(solution)/shard_map/ppermute | solution.py:376
  13.1 1.3 %collective-permute-start.2 = (f32[33,8,256]{2,1,0:T(8,128)S(1)}, f32[33,8,256]{2,1,0:T(8,128)S(1)}, u32[]{:S(2)}, u32[]{:S(2)}) collective-permute-start(f32[33,8,256]{2,1,0:T(8,128)S(1)} %pad_maximum_fusion.3), channel_id=1, source_target_pairs={{8,0},{16,8},{24,16},{9,1},{17,9},{25,17},{10,2},{18,10},{26,18},{... | collective-permute-start | bytes 811016 | tf_op jit(solution)/shard_map/ppermute | solution.py:376
  14.4 4.8 %collective-permute-start.6 = (f32[3,64,256]{2,1,0:T(8,128)S(1)}, f32[3,64,256]{2,1,0:T(8,128)S(1)}, u32[]{:S(2)}, u32[]{:S(2)}) collective-permute-start(f32[3,64,256]{2,1,0:T(8,128)S(1)} %add.230), channel_id=1, source_target_pairs={{0,16},{8,24},{16,0},{24,8},{1,17},{9,25},{17,1},{25,9},{2,18},{10... | collective-permute-start | bytes 589832 | tf_op jit(solution)/shard_map/ppermute | solution.py:27
  19.3 1.6 %collective-permute-start.5 = (f32[3,64,256]{2,1,0:T(8,128)S(1)}, f32[3,64,256]{2,1,0:T(8,128)S(1)}, u32[]{:S(2)}, u32[]{:S(2)}) collective-permute-start(f32[3,64,256]{2,1,0:T(8,128)S(1)} %add.229), channel_id=1, source_target_pairs={{0,4},{1,5},{2,6},{3,7},{4,0},{5,1},{6,2},{7,3},{8,12},{9,13},{10,... | collective-permute-start | bytes 589832 | tf_op jit(solution)/shard_map/ppermute | solution.py:27
  20.9 0.6 fusion.74
  23.4 0.6 fusion.6
  24.1 1.7 %maximum_multiply_fusion.refs_5_ = f32[3,36,20,256]{3,2,1,0:T(8,128)} fusion(f32[1,36,20,256]{3,2,1,0:T(8,128)S(1)} %get-tuple-element.124, f32[1,36,20,256]{3,2,1,0:T(8,128)S(1)} %get-tuple-element.123, f32[1,36,20,256]{3,2,1,0:T(8,128)S(1)} %get-tuple-element.122), kind=kLoop, calls=%fused_computation | loop fusion | flops 1658880 | bytes 4423680 | tf_op jit(solution)/shard_map/div | solution.py:434
  25.8 7.4 %collective-permute-done.6 = f32[3,64,256]{2,1,0:T(8,128)S(1)} collective-permute-done((f32[3,64,256]{2,1,0:T(8,128)S(1)}, f32[3,64,256]{2,1,0:T(8,128)S(1)}, u32[]{:S(2)}, u32[]{:S(2)}) %collective-permute-start.6) | collective-permute-done | bytes 196640 | tf_op jit(solution)/shard_map/ppermute | solution.py:27
  33.4 0.6 collective-permute-start.8
  34.2 0.2 copy.29
  34.9 1.3 %fusion.64 = (f32[32,2,8,256]{3,2,1,0:T(8,128)S(1)}, f32[32,2,8,256]{3,2,1,0:T(8,128)S(1)}) fusion(f32[32,16,8,256]{3,2,1,0:T(8,128)} %refs_0_.1), kind=kLoop, calls=%fused_computation.127 | loop fusion | bytes 2097152 | tf_op jit(solution)/shard_map/slice | solution.py:447
  36.4 2.6 %collective-permute-done.7 = f32[3,64,256]{2,1,0:T(8,128)S(1)} collective-permute-done((f32[3,64,256]{2,1,0:T(8,128)S(1)}, f32[3,64,256]{2,1,0:T(8,128)S(1)}, u32[]{:S(2)}, u32[]{:S(2)}) %collective-permute-start.7) | collective-permute-done | bytes 196640 | tf_op jit(solution)/shard_map/ppermute | solution.py:27
  39.2 1.6 %collective-permute-start.12 = (f32[3,64,256]{2,1,0:T(8,128)S(1)}, f32[3,64,256]{2,1,0:T(8,128)S(1)}, u32[]{:S(2)}, u32[]{:S(2)}) collective-permute-start(f32[3,64,256]{2,1,0:T(8,128)S(1)} %add.252), channel_id=1, source_target_pairs={{0,4},{1,5},{2,6},{3,7},{4,0},{5,1},{6,2},{7,3},{8,12},{9,13},{10,... | collective-permute-start | bytes 589832 | tf_op jit(solution)/shard_map/ppermute | solution.py:27
  40.8 0.7 fusion.73
  43.0 2.6 %collective-permute-start.10 = (f32[38,2,8,256]{3,2,1,0:T(8,128)S(1)}, f32[38,2,8,256]{3,2,1,0:T(8,128)S(1)}, u32[]{:S(2)}, u32[]{:S(2)}) collective-permute-start(f32[38,2,8,256]{3,2,1,0:T(8,128)S(1)} %pad_maximum_fusion.1), channel_id=1, source_target_pairs={{1,0},{2,1},{3,2},{4,3},{5,4},{6,5},{7,6},{0,7},{9,8},{10,9},{11,1... | collective-permute-start | bytes 1867784 | tf_op jit(solution)/shard_map/ppermute | solution.py:376
  45.7 0.3 fusion.23.refs_4_
  46.0 0.5 fusion.30
  46.6 1.8 %collective-permute-done.11 = f32[3,64,256]{2,1,0:T(8,128)S(1)} collective-permute-done((f32[3,64,256]{2,1,0:T(8,128)S(1)}, f32[3,64,256]{2,1,0:T(8,128)S(1)}, u32[]{:S(2)}, u32[]{:S(2)}) %collective-permute-start.11) | collective-permute-done | bytes 196640 | tf_op jit(solution)/shard_map/ppermute | solution.py:27
  48.5 0.5 collective-permute-start.14
  49.0 0.9 collective-permute-done.13.refs_2_
  50.0 0.3 collective-permute-done.14.refs_3_
  50.3 26.2 %shard_map.101.refs_7_ = bf16[3,5,256,256]{3,2,1,0:T(8,128)(2,1)S(1)} custom-call(f32[3,64,256]{2,1,0:T(8,128)S(1)} %add.253.refs_0_, f32[3,64,256]{2,1,0:T(8,128)S(1)} %add.254.refs_1_, f32[3,64,256]{2,1,0:T(8,128)S(1)} %collective-permute-done.13.refs_2_, f32[3,64,256]{2,1,0:T(8,128)S(1)} %collective-permute-done.14.refs_3_, ...), custom_call_target="tpu_custom_call" | custom-call | flops 3019898880 | bytes 6291456 | tf_op jit(solution)/shard_map/pallas_call | solution.py:235
  76.5 1.3 %copy-done = bf16[3,5,256,256]{3,2,1,0:T(8,128)(2,1)} copy-done((bf16[3,5,256,256]{3,2,1,0:T(8,128)(2,1)}, bf16[3,5,256,256]{3,2,1,0:T(8,128)(2,1)S(1)}, u32[]{:S(2)}) %copy-start) | copy-done | bytes 1966104
  77.8 0.8 copy-done.5
  78.7 0.8 copy-done.6
  79.5 34.6 %shard_map.102 = f32[32,16,8,256]{3,2,1,0:T(8,128)} custom-call(f32[32,16,8,256]{3,2,1,0:T(8,128)} %refs_0_.1, f32[33,8,256]{2,1,0:T(8,128)} %copy-done.2, f32[33,8,256]{2,1,0:T(8,128)} %copy-done.3, f32[38,2,8,256]{3,2,1,0:T(8,128)} %copy-done.5, f32[38,2,8,256]{3,2,1,0:T(8,128)} %copy-done.6, f32[3,36,20,256]{3,2,1,0:T(8,128)} %maximum_multiply_fusion.refs_5_, ...), custom_call_target="tpu_custom_call" | custom-call | tf_op jit(solution)/shard_map/pallas_call | solution.py:348
  (101 shorter events, 2.6 us)
Async XLA Ops:
  0.0 8.8 %copy-start.7 = (f32[32,16,8]{0,2,1:T(8,128)S(1)}, f32[32,16,8]{0,2,1:T(8,128)}, u32[]{:S(2)}) copy-start(f32[32,16,8]{0,2,1:T(8,128)} %param.19) | copy-start | bytes 49156
  0.0 8.8 %copy-start.8 = (f32[32,16,8]{0,2,1:T(8,128)S(1)}, f32[32,16,8]{0,2,1:T(8,128)}, u32[]{:S(2)}) copy-start(f32[32,16,8]{0,2,1:T(8,128)} %param.18) | copy-start | bytes 49156
  0.0 8.8 %copy-start.9 = (f32[32,16,8]{0,2,1:T(8,128)S(1)}, f32[32,16,8]{0,2,1:T(8,128)}, u32[]{:S(2)}) copy-start(f32[32,16,8]{0,2,1:T(8,128)} %param.17) | copy-start | bytes 49156
  2.3 1.9 %collective-permute-start = (f32[2,3,64,256]{3,2,1,0:T(8,128)S(1)}, f32[2,3,64,256]{3,2,1,0:T(8,128)S(1)}, u32[]{:S(2)}, u32[]{:S(2)}) collective-permute-start(f32[2,3,64,256]{3,2,1,0:T(8,128)S(1)} %get-tuple-element.46), channel_id=1, source_target_pairs={{0,1},{1,0},{2,3},{3,2},{4,5},{5,4},{6,7},{7,6},{8,9},{9,8},{10,11... | collective-permute-start | bytes 1179656 | tf_op jit(solution)/shard_map/ppermute | solution.py:27
  4.2 16.6 %copy-start.14 = (s32[3,2]{0,1:T(2,128)S(1)}, s32[3,2]{0,1:T(2,128)}, u32[]{:S(2)}) copy-start(s32[3,2]{0,1:T(2,128)} %param.15) | copy-start | bytes 76
  4.3 16.6 %copy-start.11 = (s32[3]{0:T(128)S(1)}, s32[3]{0:T(128)}, u32[]{:S(2)}) copy-start(s32[3]{0:T(128)} %param.16) | copy-start | bytes 40
  4.3 19.0 %copy-start.10 = (s32[3,256]{1,0:T(4,128)S(1)}, s32[3,256]{1,0:T(4,128)}, u32[]{:S(2)}) copy-start(s32[3,256]{1,0:T(4,128)} %cells_hbm.1) | copy-start | bytes 9220
  4.3 19.0 %slice-start.1 = ((s32[3,256]{1,0:T(4,128)}), s32[3,128]{1,0:T(4,128)S(1)}, s32[]{:S(2)}) async-start(s32[3,256]{1,0:T(4,128)} %cells_hbm.1), calls=%async_computation.1 | async-start | bytes 4096 | tf_op jit(solution)/shard_map/slice | solution.py:403
  4.3 10.1 %collective-permute-start.4 = (f32[3,64,256]{2,1,0:T(8,128)S(1)}, f32[3,64,256]{2,1,0:T(8,128)S(1)}, u32[]{:S(2)}, u32[]{:S(2)}) collective-permute-start(f32[3,64,256]{2,1,0:T(8,128)S(1)} %get-tuple-element.52), channel_id=1, source_target_pairs={{0,8},{8,0},{16,24},{24,16},{1,9},{9,1},{17,25},{25,17},{2,10},{10... | collective-permute-start | bytes 589832 | tf_op jit(solution)/shard_map/ppermute | solution.py:27
  8.5 10.8 %collective-permute-start.3 = (f32[3,64,256]{2,1,0:T(8,128)S(1)}, f32[3,64,256]{2,1,0:T(8,128)S(1)}, u32[]{:S(2)}, u32[]{:S(2)}) collective-permute-start(f32[3,64,256]{2,1,0:T(8,128)S(1)} %get-tuple-element.51), channel_id=1, source_target_pairs={{0,2},{1,3},{2,0},{3,1},{4,6},{5,7},{6,4},{7,5},{8,10},{9,11},{10,... | collective-permute-start | bytes 589832 | tf_op jit(solution)/shard_map/ppermute | solution.py:27
  10.7 23.3 %collective-permute-start.1 = (f32[33,8,256]{2,1,0:T(8,128)S(1)}, f32[33,8,256]{2,1,0:T(8,128)S(1)}, u32[]{:S(2)}, u32[]{:S(2)}) collective-permute-start(f32[33,8,256]{2,1,0:T(8,128)S(1)} %pad_maximum_fusion.2), channel_id=1, source_target_pairs={{0,8},{8,16},{16,24},{1,9},{9,17},{17,25},{2,10},{10,18},{18,26},{... | collective-permute-start | bytes 811016 | tf_op jit(solution)/shard_map/ppermute | solution.py:376
  13.1 20.9 %collective-permute-start.2 = (f32[33,8,256]{2,1,0:T(8,128)S(1)}, f32[33,8,256]{2,1,0:T(8,128)S(1)}, u32[]{:S(2)}, u32[]{:S(2)}) collective-permute-start(f32[33,8,256]{2,1,0:T(8,128)S(1)} %pad_maximum_fusion.3), channel_id=1, source_target_pairs={{8,0},{16,8},{24,16},{9,1},{17,9},{25,17},{10,2},{18,10},{26,18},{... | collective-permute-start | bytes 811016 | tf_op jit(solution)/shard_map/ppermute | solution.py:376
  14.4 18.8 %collective-permute-start.6 = (f32[3,64,256]{2,1,0:T(8,128)S(1)}, f32[3,64,256]{2,1,0:T(8,128)S(1)}, u32[]{:S(2)}, u32[]{:S(2)}) collective-permute-start(f32[3,64,256]{2,1,0:T(8,128)S(1)} %add.230), channel_id=1, source_target_pairs={{0,16},{8,24},{16,0},{24,8},{1,17},{9,25},{17,1},{25,9},{2,18},{10... | collective-permute-start | bytes 589832 | tf_op jit(solution)/shard_map/ppermute | solution.py:27
  19.3 14.0 %collective-permute-start.5 = (f32[3,64,256]{2,1,0:T(8,128)S(1)}, f32[3,64,256]{2,1,0:T(8,128)S(1)}, u32[]{:S(2)}, u32[]{:S(2)}) collective-permute-start(f32[3,64,256]{2,1,0:T(8,128)S(1)} %add.229), channel_id=1, source_target_pairs={{0,4},{1,5},{2,6},{3,7},{4,0},{5,1},{6,2},{7,3},{8,12},{9,13},{10,... | collective-permute-start | bytes 589832 | tf_op jit(solution)/shard_map/ppermute | solution.py:27
  33.3 5.7 %collective-permute-start.7 = (f32[3,64,256]{2,1,0:T(8,128)S(1)}, f32[3,64,256]{2,1,0:T(8,128)S(1)}, u32[]{:S(2)}, u32[]{:S(2)}) collective-permute-start(f32[3,64,256]{2,1,0:T(8,128)S(1)} %add.231), channel_id=1, source_target_pairs={{0,8},{8,0},{16,24},{24,16},{1,9},{9,1},{17,25},{25,17},{2,10},{10... | collective-permute-start | bytes 589832 | tf_op jit(solution)/shard_map/ppermute | solution.py:27
  33.4 5.7 %collective-permute-start.8 = (f32[3,64,256]{2,1,0:T(8,128)S(1)}, f32[3,64,256]{2,1,0:T(8,128)S(1)}, u32[]{:S(2)}, u32[]{:S(2)}) collective-permute-start(f32[3,64,256]{2,1,0:T(8,128)S(1)} %add.232), channel_id=1, source_target_pairs={{0,2},{1,3},{2,0},{3,1},{4,6},{5,7},{6,4},{7,5},{8,10},{9,11},{10,... | collective-permute-start | bytes 589832 | tf_op jit(solution)/shard_map/ppermute | solution.py:27
  34.0 2.4 %copy-start.2 = (f32[33,8,256]{2,1,0:T(8,128)}, f32[33,8,256]{2,1,0:T(8,128)S(1)}, u32[]{:S(2)}) copy-start(f32[33,8,256]{2,1,0:T(8,128)S(1)} %collective-permute-done.1.refs_1_) | copy-start | bytes 811012
  34.0 2.4 %copy-start.3 = (f32[33,8,256]{2,1,0:T(8,128)}, f32[33,8,256]{2,1,0:T(8,128)S(1)}, u32[]{:S(2)}) copy-start(f32[33,8,256]{2,1,0:T(8,128)S(1)} %collective-permute-done.2.refs_2_) | copy-start | bytes 811012
  34.8 4.2 %copy-start.4 = (f32[3,16,8,128]{3,2,1,0:T(8,128)}, f32[3,16,8,128]{3,2,1,0:T(8,128)S(1)}, u32[]{:S(2)}) copy-start(f32[3,16,8,128]{3,2,1,0:T(8,128)S(1)} %select_maximum_fusion.refs_6_) | copy-start | bytes 589828
  34.9 7.9 %slice-start.2 = ((s32[3,256]{1,0:T(4,128)}), s32[3,128]{1,0:T(4,128)S(1)}, s32[]{:S(2)}) async-start(s32[3,256]{1,0:T(4,128)} %cells_hbm.1), calls=%async_computation.2 | async-start | bytes 4096 | tf_op jit(solution)/shard_map/slice | solution.py:403
  36.2 9.4 %copy-start.12 = (f32[3,256]{1,0:T(4,128)S(1)}, f32[3,256]{1,0:T(4,128)}, u32[]{:S(2)}) copy-start(f32[3,256]{1,0:T(4,128)} %param.13) | copy-start | bytes 9220
  36.2 9.4 %slice-start.3 = ((f32[3,256]{1,0:T(4,128)}), f32[3,128]{1,0:T(4,128)S(1)}, s32[]{:S(2)}) async-start(f32[3,256]{1,0:T(4,128)} %param.13), calls=%async_computation.3 | async-start | bytes 4096 | tf_op jit(solution)/shard_map/slice | solution.py:403
  36.3 9.4 %copy-start.13 = (f32[3,256]{1,0:T(4,128)S(1)}, f32[3,256]{1,0:T(4,128)}, u32[]{:S(2)}) copy-start(f32[3,256]{1,0:T(4,128)} %param.11) | copy-start | bytes 9220
  36.3 9.4 %slice-start.4 = ((f32[3,256]{1,0:T(4,128)}), f32[3,128]{1,0:T(4,128)S(1)}, s32[]{:S(2)}) async-start(f32[3,256]{1,0:T(4,128)} %param.11), calls=%async_computation.4 | async-start | bytes 4096 | tf_op jit(solution)/shard_map/slice | solution.py:403
  36.3 9.4 %copy-start.1 = (f32[3,256,256]{2,1,0:T(8,128)S(1)}, f32[3,256,256]{2,1,0:T(8,128)}, u32[]{:S(2)}) copy-start(f32[3,256,256]{2,1,0:T(8,128)} %param.12) | copy-start | bytes 2359300
  36.3 9.4 %slice-start = ((f32[3,256,256]{2,1,0:T(8,128)}), f32[3,128,256]{2,1,0:T(8,128)S(1)}, s32[]{:S(2)}) async-start(f32[3,256,256]{2,1,0:T(8,128)} %param.12), calls=%async_computation | async-start | bytes 786432 | tf_op jit(solution)/shard_map/slice | solution.py:403
  39.1 9.3 %collective-permute-start.11 = (f32[3,64,256]{2,1,0:T(8,128)S(1)}, f32[3,64,256]{2,1,0:T(8,128)S(1)}, u32[]{:S(2)}, u32[]{:S(2)}) collective-permute-start(f32[3,64,256]{2,1,0:T(8,128)S(1)} %add.251), channel_id=1, source_target_pairs={{0,16},{8,24},{16,0},{24,8},{1,17},{9,25},{17,1},{25,9},{2,18},{10... | collective-permute-start | bytes 589832 | tf_op jit(solution)/shard_map/ppermute | solution.py:27
  39.2 9.2 %collective-permute-start.12 = (f32[3,64,256]{2,1,0:T(8,128)S(1)}, f32[3,64,256]{2,1,0:T(8,128)S(1)}, u32[]{:S(2)}, u32[]{:S(2)}) collective-permute-start(f32[3,64,256]{2,1,0:T(8,128)S(1)} %add.252), channel_id=1, source_target_pairs={{0,4},{1,5},{2,6},{3,7},{4,0},{5,1},{6,2},{7,3},{8,12},{9,13},{10,... | collective-permute-start | bytes 589832 | tf_op jit(solution)/shard_map/ppermute | solution.py:27
  43.0 34.8 %collective-permute-start.9 = (f32[38,2,8,256]{3,2,1,0:T(8,128)S(1)}, f32[38,2,8,256]{3,2,1,0:T(8,128)S(1)}, u32[]{:S(2)}, u32[]{:S(2)}) collective-permute-start(f32[38,2,8,256]{3,2,1,0:T(8,128)S(1)} %pad_maximum_fusion), channel_id=1, source_target_pairs={{0,1},{1,2},{2,3},{3,4},{4,5},{5,6},{6,7},{7,0},{8,9},{9,10},{10,1... | collective-permute-start | bytes 1867784 | tf_op jit(solution)/shard_map/ppermute | solution.py:376
  43.0 34.8 %collective-permute-start.10 = (f32[38,2,8,256]{3,2,1,0:T(8,128)S(1)}, f32[38,2,8,256]{3,2,1,0:T(8,128)S(1)}, u32[]{:S(2)}, u32[]{:S(2)}) collective-permute-start(f32[38,2,8,256]{3,2,1,0:T(8,128)S(1)} %pad_maximum_fusion.1), channel_id=1, source_target_pairs={{1,0},{2,1},{3,2},{4,3},{5,4},{6,5},{7,6},{0,7},{9,8},{10,9},{11,1... | collective-permute-start | bytes 1867784 | tf_op jit(solution)/shard_map/ppermute | solution.py:376
  48.5 1.5 %collective-permute-start.13 = (f32[3,64,256]{2,1,0:T(8,128)S(1)}, f32[3,64,256]{2,1,0:T(8,128)S(1)}, u32[]{:S(2)}, u32[]{:S(2)}) collective-permute-start(f32[3,64,256]{2,1,0:T(8,128)S(1)} %add.253.refs_0_), channel_id=1, source_target_pairs={{0,1},{1,0},{2,3},{3,2},{4,5},{5,4},{6,7},{7,6},{8,9},{9,8},{10,11... | collective-permute-start | bytes 589832 | tf_op jit(solution)/shard_map/ppermute | solution.py:27
  48.5 1.7 %collective-permute-start.14 = (f32[3,64,256]{2,1,0:T(8,128)S(1)}, f32[3,64,256]{2,1,0:T(8,128)S(1)}, u32[]{:S(2)}, u32[]{:S(2)}) collective-permute-start(f32[3,64,256]{2,1,0:T(8,128)S(1)} %add.254.refs_1_), channel_id=1, source_target_pairs={{0,1},{1,0},{2,3},{3,2},{4,5},{5,4},{6,7},{7,6},{8,9},{9,8},{10,11... | collective-permute-start | bytes 589832 | tf_op jit(solution)/shard_map/ppermute | solution.py:27
  (3 other events, 3.0 us)

commit v4 on v3

--- a/solution.py
+++ b/solution.py
@@ -361,8 +361,8 @@
             pltpu.SemaphoreType.DMA((10 + 2 * HALO + 6,)),
             pltpu.SemaphoreType.DMA,
         ],
-        compiler_params=pltpu.CompilerParams(vmem_limit_bytes=60 << 20),
-    )(*map(in_hbm, (*pieces, tapers, coefs, factors)))
+        compiler_params=pltpu.CompilerParams(vmem_limit_bytes=50 << 20),
+    )(*map(in_hbm, pieces[:3]), *pieces[3:], in_hbm(tapers), in_hbm(coefs), factors)
 
 
 def lanes(x, count):

time: 114 us -> 111 us (0.974)
  local copies, waits for them, and re-layouts: 8.12 us -> 5.12 us
    unnamed x30 -> x24, local copies, waits for them, and re-layouts: 3.03 us -> 0.06 us
  transfers between devices with their start and end apart: 15 -> 15, of which waited for: 6 -> 6; matrix products, arithmetic and copies ran while one was open for 8% -> 8% of each run, Pallas kernels for 23% -> 24%
where the time goes in v4:
time: 111 us; the launch traced here: 110 us
  Pallas kernels  62.2 us (56%)
  starting transfers between devices  20.7 us (19%)
  waiting for transfers between devices  14.4 us (13%)
  local copies, waits for them, and re-layouts  5.12 us (5%)
  other arithmetic  4.14 us (4%)
  between operations  3.82 us (3%)
    pallas_call x1, Pallas kernels, move(): pl.pallas_call(functools.partial(move_kernel, 12 if tall % 12 == 0 else 1...  33.7 us
    pallas_call x1, Pallas kernels, solve(): pl.pallas_call(solve_kernel, out_shape=jax.ShapeDtypeStruct(out, BF16), i...  26.2 us
    ppermute x11, waiting for transfers between devices, shifted(): return lax.ppermute(x, axis, [(i, i ^ flip) for i in range(size)])  14.4 us
    ppermute x11, starting transfers between devices, shifted(): return lax.ppermute(x, axis, [(i, i ^ flip) for i in range(size)])  14.4 us
    ppermute x4, starting transfers between devices, neighbours(): return (lax.ppermute(before, axis, up), lax.ppermute(after, axis, down))  6.3 us
    pallas_call x1, Pallas kernels, gather(): pl.pallas_call(gather_kernel, out_shape=[out, out], in_specs=[HBM] * 3, o...  2.26 us
  transfers between devices with their start and end apart: 15, of which 6 were waited for; matrix products, arithmetic and copies ran while one was open for 8% of the time, Pallas kernels for 24%

profile of v4, /device:TPU:0, one launch (start us, length us, event | category | flops | bytes accessed | tf_op | source)
XLA Modules:
  0.0 110.4 jit_solution(12029038392162763234)
XLA Ops:
  0.0 2.3 %shard_map.100 = (f32[2,3,64,256]{3,2,1,0:T(8,128)S(1)}, f32[2,3,64,256]{3,2,1,0:T(8,128)S(1)}) custom-call(s32[3,256]{1,0:T(4,128)} %cells_hbm.1, s32[2,3]{1,0:T(2,128)} %bitcast.78, f32[4096,256]{1,0:T(8,128)} %bitcast.62), custom_call_target="tpu_custom_call" | custom-call | tf_op jit(solution)/shard_map/pallas_call | solution.py:71
  2.3 0.6 collective-permute-start
  2.8 1.3 %collective-permute-done = f32[2,3,64,256]{3,2,1,0:T(8,128)S(1)} collective-permute-done((f32[2,3,64,256]{3,2,1,0:T(8,128)S(1)}, f32[2,3,64,256]{3,2,1,0:T(8,128)S(1)}, u32[]{:S(2)}, u32[]{:S(2)}) %collective-permute-start) | collective-permute-done | bytes 393248 | tf_op jit(solution)/shard_map/ppermute | solution.py:27
  4.3 4.3 %collective-permute-start.4 = (f32[3,64,256]{2,1,0:T(8,128)S(1)}, f32[3,64,256]{2,1,0:T(8,128)S(1)}, u32[]{:S(2)}, u32[]{:S(2)}) collective-permute-start(f32[3,64,256]{2,1,0:T(8,128)S(1)} %get-tuple-element.52), channel_id=1, source_target_pairs={{0,8},{8,0},{16,24},{24,16},{1,9},{9,1},{17,25},{25,17},{2,10},{10... | collective-permute-start | bytes 589832 | tf_op jit(solution)/shard_map/ppermute | solution.py:27
  8.6 0.2 collective-permute-start.3
  8.9 0.2 copy.25
  9.2 0.2 copy.23
  9.6 1.1 fusion.65
  10.7 2.4 %collective-permute-start.1 = (f32[33,8,256]{2,1,0:T(8,128)S(1)}, f32[33,8,256]{2,1,0:T(8,128)S(1)}, u32[]{:S(2)}, u32[]{:S(2)}) collective-permute-start(f32[33,8,256]{2,1,0:T(8,128)S(1)} %pad_maximum_fusion.2), channel_id=1, source_target_pairs={{0,8},{8,16},{16,24},{1,9},{9,17},{17,25},{2,10},{10,18},{18,26},{... | collective-permute-start | bytes 811016 | tf_op jit(solution)/shard_map/ppermute | solution.py:376
  13.1 1.3 %collective-permute-start.2 = (f32[33,8,256]{2,1,0:T(8,128)S(1)}, f32[33,8,256]{2,1,0:T(8,128)S(1)}, u32[]{:S(2)}, u32[]{:S(2)}) collective-permute-start(f32[33,8,256]{2,1,0:T(8,128)S(1)} %pad_maximum_fusion.3), channel_id=1, source_target_pairs={{8,0},{16,8},{24,16},{9,1},{17,9},{25,17},{10,2},{18,10},{26,18},{... | collective-permute-start | bytes 811016 | tf_op jit(solution)/shard_map/ppermute | solution.py:376
  14.4 4.8 %collective-permute-start.6 = (f32[3,64,256]{2,1,0:T(8,128)S(1)}, f32[3,64,256]{2,1,0:T(8,128)S(1)}, u32[]{:S(2)}, u32[]{:S(2)}) collective-permute-start(f32[3,64,256]{2,1,0:T(8,128)S(1)} %add.230), channel_id=1, source_target_pairs={{0,16},{8,24},{16,0},{24,8},{1,17},{9,25},{17,1},{25,9},{2,18},{10... | collective-permute-start | bytes 589832 | tf_op jit(solution)/shard_map/ppermute | solution.py:27
  19.3 1.6 %collective-permute-start.5 = (f32[3,64,256]{2,1,0:T(8,128)S(1)}, f32[3,64,256]{2,1,0:T(8,128)S(1)}, u32[]{:S(2)}, u32[]{:S(2)}) collective-permute-start(f32[3,64,256]{2,1,0:T(8,128)S(1)} %add.229), channel_id=1, source_target_pairs={{0,4},{1,5},{2,6},{3,7},{4,0},{5,1},{6,2},{7,3},{8,12},{9,13},{10,... | collective-permute-start | bytes 589832 | tf_op jit(solution)/shard_map/ppermute | solution.py:27
  20.9 0.6 fusion.74
  23.6 0.6 fusion.6
  24.3 1.8 %maximum_multiply_fusion.refs_5_ = f32[3,36,20,256]{3,2,1,0:T(8,128)} fusion(f32[1,36,20,256]{3,2,1,0:T(8,128)S(1)} %get-tuple-element.124, f32[1,36,20,256]{3,2,1,0:T(8,128)S(1)} %get-tuple-element.123, f32[1,36,20,256]{3,2,1,0:T(8,128)S(1)} %get-tuple-element.122), kind=kLoop, calls=%fused_computation | loop fusion | flops 1658880 | bytes 4423680 | tf_op jit(solution)/shard_map/div | solution.py:434
  26.0 7.2 %collective-permute-done.6 = f32[3,64,256]{2,1,0:T(8,128)S(1)} collective-permute-done((f32[3,64,256]{2,1,0:T(8,128)S(1)}, f32[3,64,256]{2,1,0:T(8,128)S(1)}, u32[]{:S(2)}, u32[]{:S(2)}) %collective-permute-start.6) | collective-permute-done | bytes 196640 | tf_op jit(solution)/shard_map/ppermute | solution.py:27
  33.4 0.6 collective-permute-start.8
  34.2 0.2 copy.29
  34.4 0.2 copy.30
  34.9 1.3 %fusion.64 = (f32[32,2,8,256]{3,2,1,0:T(8,128)S(1)}, f32[32,2,8,256]{3,2,1,0:T(8,128)S(1)}) fusion(f32[32,16,8,256]{3,2,1,0:T(8,128)} %refs_0_.1), kind=kLoop, calls=%fused_computation.127 | loop fusion | bytes 2097152 | tf_op jit(solution)/shard_map/slice | solution.py:447
  36.4 2.6 %collective-permute-done.7 = f32[3,64,256]{2,1,0:T(8,128)S(1)} collective-permute-done((f32[3,64,256]{2,1,0:T(8,128)S(1)}, f32[3,64,256]{2,1,0:T(8,128)S(1)}, u32[]{:S(2)}, u32[]{:S(2)}) %collective-permute-start.7) | collective-permute-done | bytes 196640 | tf_op jit(solution)/shard_map/ppermute | solution.py:27
  39.2 1.6 %collective-permute-start.12 = (f32[3,64,256]{2,1,0:T(8,128)S(1)}, f32[3,64,256]{2,1,0:T(8,128)S(1)}, u32[]{:S(2)}, u32[]{:S(2)}) collective-permute-start(f32[3,64,256]{2,1,0:T(8,128)S(1)} %add.252), channel_id=1, source_target_pairs={{0,4},{1,5},{2,6},{3,7},{4,0},{5,1},{6,2},{7,3},{8,12},{9,13},{10,... | collective-permute-start | bytes 589832 | tf_op jit(solution)/shard_map/ppermute | solution.py:27
  40.8 0.6 fusion.73
  42.8 2.6 %collective-permute-start.10 = (f32[38,2,8,256]{3,2,1,0:T(8,128)S(1)}, f32[38,2,8,256]{3,2,1,0:T(8,128)S(1)}, u32[]{:S(2)}, u32[]{:S(2)}) collective-permute-start(f32[38,2,8,256]{3,2,1,0:T(8,128)S(1)} %pad_maximum_fusion.1), channel_id=1, source_target_pairs={{1,0},{2,1},{3,2},{4,3},{5,4},{6,5},{7,6},{0,7},{9,8},{10,9},{11,1... | collective-permute-start | bytes 1867784 | tf_op jit(solution)/shard_map/ppermute | solution.py:376
  45.5 0.3 fusion.23.refs_4_
  45.7 0.5 fusion.30
  46.3 2.1 %collective-permute-done.11 = f32[3,64,256]{2,1,0:T(8,128)S(1)} collective-permute-done((f32[3,64,256]{2,1,0:T(8,128)S(1)}, f32[3,64,256]{2,1,0:T(8,128)S(1)}, u32[]{:S(2)}, u32[]{:S(2)}) %collective-permute-start.11) | collective-permute-done | bytes 196640 | tf_op jit(solution)/shard_map/ppermute | solution.py:27
  48.5 0.5 collective-permute-start.14
  49.0 0.9 collective-permute-done.13.refs_2_
  50.0 0.3 collective-permute-done.14.refs_3_
  50.3 26.2 %shard_map.101.refs_7_ = bf16[3,5,256,256]{3,2,1,0:T(8,128)(2,1)S(1)} custom-call(f32[3,64,256]{2,1,0:T(8,128)S(1)} %add.253.refs_0_, f32[3,64,256]{2,1,0:T(8,128)S(1)} %add.254.refs_1_, f32[3,64,256]{2,1,0:T(8,128)S(1)} %collective-permute-done.13.refs_2_, f32[3,64,256]{2,1,0:T(8,128)S(1)} %collective-permute-done.14.refs_3_, ...), custom_call_target="tpu_custom_call" | custom-call | flops 3019898880 | bytes 6291456 | tf_op jit(solution)/shard_map/pallas_call | solution.py:235
  76.5 33.7 %shard_map.102 = f32[32,16,8,256]{3,2,1,0:T(8,128)} custom-call(f32[32,16,8,256]{3,2,1,0:T(8,128)} %refs_0_.1, f32[33,8,256]{2,1,0:T(8,128)} %copy-done.1, f32[33,8,256]{2,1,0:T(8,128)} %copy-done.2, f32[38,2,8,256]{3,2,1,0:T(8,128)S(1)} %collective-permute-done.9.refs_3_, f32[38,2,8,256]{3,2,1,0:T(8,128)S(1)} %collective-permute-done.10.refs_4_, ...), custom_call_target="tpu_custom_call" | custom-call | tf_op jit(solution)/shard_map/pallas_call | solution.py:348
  (95 shorter events, 1.9 us)
Async XLA Ops:
  0.0 8.8 %copy-start.4 = (f32[32,16,8]{0,2,1:T(8,128)S(1)}, f32[32,16,8]{0,2,1:T(8,128)}, u32[]{:S(2)}) copy-start(f32[32,16,8]{0,2,1:T(8,128)} %param.19) | copy-start | bytes 49156
  0.0 8.8 %copy-start.5 = (f32[32,16,8]{0,2,1:T(8,128)S(1)}, f32[32,16,8]{0,2,1:T(8,128)}, u32[]{:S(2)}) copy-start(f32[32,16,8]{0,2,1:T(8,128)} %param.18) | copy-start | bytes 49156
  0.0 8.8 %copy-start.6 = (f32[32,16,8]{0,2,1:T(8,128)S(1)}, f32[32,16,8]{0,2,1:T(8,128)}, u32[]{:S(2)}) copy-start(f32[32,16,8]{0,2,1:T(8,128)} %param.17) | copy-start | bytes 49156
  2.3 1.9 %collective-permute-start = (f32[2,3,64,256]{3,2,1,0:T(8,128)S(1)}, f32[2,3,64,256]{3,2,1,0:T(8,128)S(1)}, u32[]{:S(2)}, u32[]{:S(2)}) collective-permute-start(f32[2,3,64,256]{3,2,1,0:T(8,128)S(1)} %get-tuple-element.46), channel_id=1, source_target_pairs={{0,1},{1,0},{2,3},{3,2},{4,5},{5,4},{6,7},{7,6},{8,9},{9,8},{10,11... | collective-permute-start | bytes 1179656 | tf_op jit(solution)/shard_map/ppermute | solution.py:27
  4.2 16.6 %copy-start.11 = (s32[3,2]{0,1:T(2,128)S(1)}, s32[3,2]{0,1:T(2,128)}, u32[]{:S(2)}) copy-start(s32[3,2]{0,1:T(2,128)} %param.15) | copy-start | bytes 76
  4.3 16.6 %copy-start.8 = (s32[3]{0:T(128)S(1)}, s32[3]{0:T(128)}, u32[]{:S(2)}) copy-start(s32[3]{0:T(128)} %param.16) | copy-start | bytes 40
  4.3 19.2 %copy-start.7 = (s32[3,256]{1,0:T(4,128)S(1)}, s32[3,256]{1,0:T(4,128)}, u32[]{:S(2)}) copy-start(s32[3,256]{1,0:T(4,128)} %cells_hbm.1) | copy-start | bytes 9220
  4.3 19.2 %slice-start.1 = ((s32[3,256]{1,0:T(4,128)}), s32[3,128]{1,0:T(4,128)S(1)}, s32[]{:S(2)}) async-start(s32[3,256]{1,0:T(4,128)} %cells_hbm.1), calls=%async_computation.1 | async-start | bytes 4096 | tf_op jit(solution)/shard_map/slice | solution.py:403
  4.3 10.1 %collective-permute-start.4 = (f32[3,64,256]{2,1,0:T(8,128)S(1)}, f32[3,64,256]{2,1,0:T(8,128)S(1)}, u32[]{:S(2)}, u32[]{:S(2)}) collective-permute-start(f32[3,64,256]{2,1,0:T(8,128)S(1)} %get-tuple-element.52), channel_id=1, source_target_pairs={{0,8},{8,0},{16,24},{24,16},{1,9},{9,1},{17,25},{25,17},{2,10},{10... | collective-permute-start | bytes 589832 | tf_op jit(solution)/shard_map/ppermute | solution.py:27
  8.6 10.7 %collective-permute-start.3 = (f32[3,64,256]{2,1,0:T(8,128)S(1)}, f32[3,64,256]{2,1,0:T(8,128)S(1)}, u32[]{:S(2)}, u32[]{:S(2)}) collective-permute-start(f32[3,64,256]{2,1,0:T(8,128)S(1)} %get-tuple-element.51), channel_id=1, source_target_pairs={{0,2},{1,3},{2,0},{3,1},{4,6},{5,7},{6,4},{7,5},{8,10},{9,11},{10,... | collective-permute-start | bytes 589832 | tf_op jit(solution)/shard_map/ppermute | solution.py:27
  10.7 23.3 %collective-permute-start.1 = (f32[33,8,256]{2,1,0:T(8,128)S(1)}, f32[33,8,256]{2,1,0:T(8,128)S(1)}, u32[]{:S(2)}, u32[]{:S(2)}) collective-permute-start(f32[33,8,256]{2,1,0:T(8,128)S(1)} %pad_maximum_fusion.2), channel_id=1, source_target_pairs={{0,8},{8,16},{16,24},{1,9},{9,17},{17,25},{2,10},{10,18},{18,26},{... | collective-permute-start | bytes 811016 | tf_op jit(solution)/shard_map/ppermute | solution.py:376
  13.1 20.9 %collective-permute-start.2 = (f32[33,8,256]{2,1,0:T(8,128)S(1)}, f32[33,8,256]{2,1,0:T(8,128)S(1)}, u32[]{:S(2)}, u32[]{:S(2)}) collective-permute-start(f32[33,8,256]{2,1,0:T(8,128)S(1)} %pad_maximum_fusion.3), channel_id=1, source_target_pairs={{8,0},{16,8},{24,16},{9,1},{17,9},{25,17},{10,2},{18,10},{26,18},{... | collective-permute-start | bytes 811016 | tf_op jit(solution)/shard_map/ppermute | solution.py:376
  14.4 18.8 %collective-permute-start.6 = (f32[3,64,256]{2,1,0:T(8,128)S(1)}, f32[3,64,256]{2,1,0:T(8,128)S(1)}, u32[]{:S(2)}, u32[]{:S(2)}) collective-permute-start(f32[3,64,256]{2,1,0:T(8,128)S(1)} %add.230), channel_id=1, source_target_pairs={{0,16},{8,24},{16,0},{24,8},{1,17},{9,25},{17,1},{25,9},{2,18},{10... | collective-permute-start | bytes 589832 | tf_op jit(solution)/shard_map/ppermute | solution.py:27
  19.3 14.0 %collective-permute-start.5 = (f32[3,64,256]{2,1,0:T(8,128)S(1)}, f32[3,64,256]{2,1,0:T(8,128)S(1)}, u32[]{:S(2)}, u32[]{:S(2)}) collective-permute-start(f32[3,64,256]{2,1,0:T(8,128)S(1)} %add.229), channel_id=1, source_target_pairs={{0,4},{1,5},{2,6},{3,7},{4,0},{5,1},{6,2},{7,3},{8,12},{9,13},{10,... | collective-permute-start | bytes 589832 | tf_op jit(solution)/shard_map/ppermute | solution.py:27
  33.3 5.7 %collective-permute-start.7 = (f32[3,64,256]{2,1,0:T(8,128)S(1)}, f32[3,64,256]{2,1,0:T(8,128)S(1)}, u32[]{:S(2)}, u32[]{:S(2)}) collective-permute-start(f32[3,64,256]{2,1,0:T(8,128)S(1)} %add.231), channel_id=1, source_target_pairs={{0,8},{8,0},{16,24},{24,16},{1,9},{9,1},{17,25},{25,17},{2,10},{10... | collective-permute-start | bytes 589832 | tf_op jit(solution)/shard_map/ppermute | solution.py:27
  33.4 5.7 %collective-permute-start.8 = (f32[3,64,256]{2,1,0:T(8,128)S(1)}, f32[3,64,256]{2,1,0:T(8,128)S(1)}, u32[]{:S(2)}, u32[]{:S(2)}) collective-permute-start(f32[3,64,256]{2,1,0:T(8,128)S(1)} %add.232), channel_id=1, source_target_pairs={{0,2},{1,3},{2,0},{3,1},{4,6},{5,7},{6,4},{7,5},{8,10},{9,11},{10,... | collective-permute-start | bytes 589832 | tf_op jit(solution)/shard_map/ppermute | solution.py:27
  34.0 2.4 %copy-start.1 = (f32[33,8,256]{2,1,0:T(8,128)}, f32[33,8,256]{2,1,0:T(8,128)S(1)}, u32[]{:S(2)}) copy-start(f32[33,8,256]{2,1,0:T(8,128)S(1)} %collective-permute-done.1.refs_1_) | copy-start | bytes 811012
  34.0 2.4 %copy-start.2 = (f32[33,8,256]{2,1,0:T(8,128)}, f32[33,8,256]{2,1,0:T(8,128)S(1)}, u32[]{:S(2)}) copy-start(f32[33,8,256]{2,1,0:T(8,128)S(1)} %collective-permute-done.2.refs_2_) | copy-start | bytes 811012
  34.8 4.2 %copy-start.3 = (f32[3,16,8,128]{3,2,1,0:T(8,128)}, f32[3,16,8,128]{3,2,1,0:T(8,128)S(1)}, u32[]{:S(2)}) copy-start(f32[3,16,8,128]{3,2,1,0:T(8,128)S(1)} %select_maximum_fusion.refs_6_) | copy-start | bytes 589828
  34.9 7.7 %slice-start.2 = ((s32[3,256]{1,0:T(4,128)}), s32[3,128]{1,0:T(4,128)S(1)}, s32[]{:S(2)}) async-start(s32[3,256]{1,0:T(4,128)} %cells_hbm.1), calls=%async_computation.2 | async-start | bytes 4096 | tf_op jit(solution)/shard_map/slice | solution.py:403
  36.2 9.2 %copy-start.9 = (f32[3,256]{1,0:T(4,128)S(1)}, f32[3,256]{1,0:T(4,128)}, u32[]{:S(2)}) copy-start(f32[3,256]{1,0:T(4,128)} %param.13) | copy-start | bytes 9220
  36.2 9.2 %slice-start.3 = ((f32[3,256]{1,0:T(4,128)}), f32[3,128]{1,0:T(4,128)S(1)}, s32[]{:S(2)}) async-start(f32[3,256]{1,0:T(4,128)} %param.13), calls=%async_computation.3 | async-start | bytes 4096 | tf_op jit(solution)/shard_map/slice | solution.py:403
  36.3 9.2 %copy-start.10 = (f32[3,256]{1,0:T(4,128)S(1)}, f32[3,256]{1,0:T(4,128)}, u32[]{:S(2)}) copy-start(f32[3,256]{1,0:T(4,128)} %param.11) | copy-start | bytes 9220
  36.3 9.1 %slice-start.4 = ((f32[3,256]{1,0:T(4,128)}), f32[3,128]{1,0:T(4,128)S(1)}, s32[]{:S(2)}) async-start(f32[3,256]{1,0:T(4,128)} %param.11), calls=%async_computation.4 | async-start | bytes 4096 | tf_op jit(solution)/shard_map/slice | solution.py:403
  36.3 9.2 %copy-start = (f32[3,256,256]{2,1,0:T(8,128)S(1)}, f32[3,256,256]{2,1,0:T(8,128)}, u32[]{:S(2)}) copy-start(f32[3,256,256]{2,1,0:T(8,128)} %param.12) | copy-start | bytes 2359300
  36.3 9.2 %slice-start = ((f32[3,256,256]{2,1,0:T(8,128)}), f32[3,128,256]{2,1,0:T(8,128)S(1)}, s32[]{:S(2)}) async-start(f32[3,256,256]{2,1,0:T(8,128)} %param.12), calls=%async_computation | async-start | bytes 786432 | tf_op jit(solution)/shard_map/slice | solution.py:403
  39.1 9.3 %collective-permute-start.11 = (f32[3,64,256]{2,1,0:T(8,128)S(1)}, f32[3,64,256]{2,1,0:T(8,128)S(1)}, u32[]{:S(2)}, u32[]{:S(2)}) collective-permute-start(f32[3,64,256]{2,1,0:T(8,128)S(1)} %add.251), channel_id=1, source_target_pairs={{0,16},{8,24},{16,0},{24,8},{1,17},{9,25},{17,1},{25,9},{2,18},{10... | collective-permute-start | bytes 589832 | tf_op jit(solution)/shard_map/ppermute | solution.py:27
  39.2 9.2 %collective-permute-start.12 = (f32[3,64,256]{2,1,0:T(8,128)S(1)}, f32[3,64,256]{2,1,0:T(8,128)S(1)}, u32[]{:S(2)}, u32[]{:S(2)}) collective-permute-start(f32[3,64,256]{2,1,0:T(8,128)S(1)} %add.252), channel_id=1, source_target_pairs={{0,4},{1,5},{2,6},{3,7},{4,0},{5,1},{6,2},{7,3},{8,12},{9,13},{10,... | collective-permute-start | bytes 589832 | tf_op jit(solution)/shard_map/ppermute | solution.py:27
  42.8 33.8 %collective-permute-start.9 = (f32[38,2,8,256]{3,2,1,0:T(8,128)S(1)}, f32[38,2,8,256]{3,2,1,0:T(8,128)S(1)}, u32[]{:S(2)}, u32[]{:S(2)}) collective-permute-start(f32[38,2,8,256]{3,2,1,0:T(8,128)S(1)} %pad_maximum_fusion), channel_id=1, source_target_pairs={{0,1},{1,2},{2,3},{3,4},{4,5},{5,6},{6,7},{7,0},{8,9},{9,10},{10,1... | collective-permute-start | bytes 1867784 | tf_op jit(solution)/shard_map/ppermute | solution.py:376
  42.8 33.7 %collective-permute-start.10 = (f32[38,2,8,256]{3,2,1,0:T(8,128)S(1)}, f32[38,2,8,256]{3,2,1,0:T(8,128)S(1)}, u32[]{:S(2)}, u32[]{:S(2)}) collective-permute-start(f32[38,2,8,256]{3,2,1,0:T(8,128)S(1)} %pad_maximum_fusion.1), channel_id=1, source_target_pairs={{1,0},{2,1},{3,2},{4,3},{5,4},{6,5},{7,6},{0,7},{9,8},{10,9},{11,1... | collective-permute-start | bytes 1867784 | tf_op jit(solution)/shard_map/ppermute | solution.py:376
  48.5 1.5 %collective-permute-start.13 = (f32[3,64,256]{2,1,0:T(8,128)S(1)}, f32[3,64,256]{2,1,0:T(8,128)S(1)}, u32[]{:S(2)}, u32[]{:S(2)}) collective-permute-start(f32[3,64,256]{2,1,0:T(8,128)S(1)} %add.253.refs_0_), channel_id=1, source_target_pairs={{0,1},{1,0},{2,3},{3,2},{4,5},{5,4},{6,7},{7,6},{8,9},{9,8},{10,11... | collective-permute-start | bytes 589832 | tf_op jit(solution)/shard_map/ppermute | solution.py:27
  48.5 1.7 %collective-permute-start.14 = (f32[3,64,256]{2,1,0:T(8,128)S(1)}, f32[3,64,256]{2,1,0:T(8,128)S(1)}, u32[]{:S(2)}, u32[]{:S(2)}) collective-permute-start(f32[3,64,256]{2,1,0:T(8,128)S(1)} %add.254.refs_1_), channel_id=1, source_target_pairs={{0,1},{1,0},{2,3},{3,2},{4,5},{5,4},{6,7},{7,6},{8,9},{9,8},{10,11... | collective-permute-start | bytes 589832 | tf_op jit(solution)/shard_map/ppermute | solution.py:27
